TPU v7x, 32 devices: a whole 2x2x4 slice. The times are simulated.
32 devices in a mesh: groups: 2 (over y), ulysses: 4 (over z), blk: 2 (over x), handoff: 2 (over core).
Axes of the slice: x: 2, y: 2, z: 4, core: 2. Of those that a mesh axis runs over, the one named last changes fastest.
Arguments:
- queries: bfloat16 [4, 512, 4096], P(('groups', 'handoff'), ('blk', 'ulysses')), parts along dimension 0, may hold values from -24 to 24
- keys: bfloat16 [4, 512, 2048], P(('groups', 'handoff'), ('blk', 'ulysses')), parts along dimension 0, may hold values from -7.5 to 7.5
- values: bfloat16 [4, 512, 2048], P(('groups', 'handoff'), ('blk', 'ulysses')), parts along dimension 0, may hold values from -6 to 6
- request_pages: int32 [4, 4], P('groups'), parts along dimension 0, may hold values from 1 to 4, 8 in all within a row
- page_table: int32 [4, 8], P('groups'), parts along dimension 0, may hold values from 0 to 15, as said below
Outputs:
- attended: bfloat16 [4, 512, 4096], P(('groups', 'handoff'), ('blk', 'ulysses')), parts along dimension 0
- cache_keys: bfloat16 [32, 16, 64, 128], P(('groups', 'blk', 'handoff'), 'ulysses'), parts along dimension 0
- cache_values: bfloat16 [32, 16, 64, 128], P(('groups', 'blk', 'handoff'), 'ulysses'), parts along dimension 0
There are 2 independent parts, one for each index of `groups`. A program takes and returns all parts, laid end to end along the dimension named above; each array names one. Nothing has to cross between parts.
Inputs may be any that keep to these rules, and one draw needn't show every extreme that they name: `request_pages`: A pack's 4 requests fill its 8 pages; the longest holds exactly 4 of them. `page_table`: all rows together name every pool page once; the 4 pages of each aligned run of 4 pages of a pack's row go in equal numbers to each aligned run of 4 pool pages.
All inputs are finite; a program needn't handle non-finite values.
Results may differ from a plain program's by a relative error of at most 0.012.
Values may be sent and summed in bfloat16 or wider, within the bound.
A program may use at most 64 MiB of HBM per device.

v0:
```python
import math

import jax
import jax.numpy as jnp
from jax import lax
from jax.sharding import PartitionSpec as P

QH = 32
KVH = 16
HD = 128
WINDOW = 4096
PAGE = 64


QUERY_SCALE = 144.0 ** (-0.5)
SOFT_CAP = 50.0
ROPE_BASE = 10000.0


def from_behind(block, axis, distance):
    devices = range(lax.axis_size(axis))
    route = [(i - distance, i) for i in devices if i - distance in devices]
    return lax.ppermute(block, axis, route)


def request_marks(pages_row, positions):
    request_ends = jnp.cumsum(pages_row, dtype=jnp.int32) * PAGE
    request_starts = request_ends - pages_row * PAGE
    owner_index = jnp.sum((positions[:, None] >= request_ends[None, :]).astype(jnp.int32), axis=1)
    first_token = jnp.max(
        jnp.where(positions[:, None] >= request_starts[None, :], request_starts[None, :], 0), axis=1
    )
    return (owner_index, positions - first_token)


def rotate(head_rows, offsets):
    head_width = head_rows.shape[-1]
    half_width = head_width // 2
    frequency = ROPE_BASE ** (-(2.0 * jnp.arange(half_width, dtype=jnp.float32)) / head_width)
    angles = offsets.astype(jnp.float32)[:, None] * frequency[None, :]
    cosine = jnp.cos(angles)[:, None, :]
    sines = jnp.sin(angles)[:, None, :]
    as_float = head_rows.astype(jnp.float32)
    front_half = as_float[..., :half_width]
    back_half = as_float[..., half_width:]
    turned = jnp.concatenate(
        [front_half * cosine - back_half * sines, back_half * cosine + front_half * sines], axis=-1
    )
    return turned.astype(jnp.bfloat16)


def body(queries, keys, values, request_pages, page_table):
    local_rows = queries.shape[1]
    ulysses_size = lax.axis_size("ulysses")
    blk_size = lax.axis_size("blk")
    core_count = lax.axis_size("handoff")
    pack_index = lax.axis_index("handoff")
    blk_index = lax.axis_index("blk")
    shard_rows = local_rows * ulysses_size
    window = WINDOW
    earlier_count = min(window // shard_rows, blk_size - 1)
    kv_local = KVH // ulysses_size
    group_size = QH // KVH
    query_split = queries[0].reshape(local_rows, ulysses_size, kv_local * group_size * HD)
    key_split = keys[0].reshape(local_rows, ulysses_size, kv_local * HD)
    value_split = values[0].reshape(local_rows, ulysses_size, kv_local * HD)
    pages_row = lax.dynamic_index_in_dim(request_pages, pack_index, 0, keepdims=False)
    positions = blk_index * shard_rows + jnp.arange(shard_rows, dtype=jnp.int32)
    query_owner, offsets = request_marks(pages_row, positions)
    queries_moved, keys_moved, values_moved = (
        lax.all_to_all(query_split, "ulysses", split_axis=1, concat_axis=0, tiled=True),
        lax.all_to_all(key_split, "ulysses", split_axis=1, concat_axis=0, tiled=True),
        lax.all_to_all(value_split, "ulysses", split_axis=1, concat_axis=0, tiled=True),
    )
    key_turned = rotate(keys_moved.reshape(shard_rows, kv_local, HD), offsets)
    local_kv = jnp.stack(
        [
            key_turned.reshape(shard_rows, kv_local * HD),
            values_moved.reshape(shard_rows, kv_local * HD),
        ]
    )
    earlier = []
    carried = local_kv
    for hop in range(earlier_count):
        carried = from_behind(carried, "blk", 1)
        earlier.append(carried)
    slots_dev = shard_rows // PAGE
    sources = blk_size * core_count
    per_peer = slots_dev // sources
    pack_row = lax.dynamic_index_in_dim(page_table, pack_index, 0, keepdims=False)
    my_pages = lax.dynamic_slice_in_dim(pack_row, blk_index * slots_dev, slots_dev)
    send_order = jnp.argsort(my_pages)
    paged = local_kv.reshape(2, slots_dev, PAGE, kv_local, HD)[:, send_order]
    paged = jnp.transpose(paged, (0, 1, 3, 2, 4))
    outgoing = paged.reshape(2, sources, per_peer, kv_local, PAGE, HD)
    received = lax.all_to_all(outgoing, ("blk", "handoff"), split_axis=1, concat_axis=1, tiled=True)
    received = received.reshape(2, slots_dev, kv_local, PAGE, HD)
    page_grid = jnp.transpose(
        page_table.reshape(core_count, blk_size, slots_dev), (1, 0, 2)
    ).reshape(sources, slots_dev)
    my_index = blk_index * core_count + pack_index
    is_here = page_grid // slots_dev == my_index
    picked = (
        jnp.sort(jnp.where(is_here, page_grid, page_table.size), axis=1)[:, :per_peer]
        - my_index * slots_dev
    )
    inverse = jnp.argsort(picked.reshape(-1))
    cache_keys = received[0][inverse]
    cache_values = received[1][inverse]
    query_turned = rotate(queries_moved.reshape(shard_rows, kv_local * group_size, HD), offsets)
    query_turned = query_turned.reshape(shard_rows, kv_local, group_size, HD)
    front_rows = window - earlier_count * shard_rows
    front_zeros = jnp.zeros((2, front_rows, kv_local * HD), jnp.bfloat16)
    table_kv = jnp.concatenate([front_zeros] + earlier[::-1] + [local_kv], axis=1)
    key_positions = (
        blk_index * shard_rows - window + jnp.arange(window + shard_rows, dtype=jnp.int32)
    )
    key_owner, unused_offsets = request_marks(pages_row, key_positions)
    block_rows = math.gcd(shard_rows, 128)
    key_span = window + block_rows

    def attend(offset):
        query_block = lax.dynamic_slice_in_dim(query_turned, offset, block_rows, 0)
        kv_block = lax.dynamic_slice_in_dim(table_kv, offset, key_span, 1)
        key_block = kv_block[0].reshape(key_span, kv_local, HD)
        value_block = kv_block[1].reshape(key_span, kv_local, HD)
        scores = (
            jnp.einsum("qgrd,kgd->gqrk", query_block, key_block, preferred_element_type=jnp.float32)
            * QUERY_SCALE
        )
        capped = SOFT_CAP * jnp.tanh(scores / SOFT_CAP)
        query_pos = lax.dynamic_slice_in_dim(positions, offset, block_rows)
        query_part = lax.dynamic_slice_in_dim(query_owner, offset, block_rows)
        key_pos = lax.dynamic_slice_in_dim(key_positions, offset, key_span)
        key_part = lax.dynamic_slice_in_dim(key_owner, offset, key_span)
        distance = query_pos[:, None] - key_pos[None, :]
        allowed = (
            (query_part[:, None] == key_part[None, :])
            & (distance >= 0)
            & (distance < window)
            & (key_pos[None, :] >= 0)
        )
        weights = jnp.where(allowed[None, :, None, :], jnp.exp(capped), jnp.float32(0.0))
        totals = jnp.sum(weights, axis=-1)
        mixture = jnp.einsum(
            "gqrk,kgd->qgrd",
            weights.astype(jnp.bfloat16),
            value_block,
            preferred_element_type=jnp.float32,
        )
        return (mixture / jnp.transpose(totals, (1, 0, 2))[..., None]).astype(jnp.bfloat16)

    starts = jnp.arange(shard_rows // block_rows, dtype=jnp.int32) * block_rows
    blocks = lax.map(attend, starts)
    outgoing_heads = blocks.reshape(ulysses_size, local_rows, 1, kv_local * group_size * HD)
    merged = lax.all_to_all(outgoing_heads, "ulysses", split_axis=0, concat_axis=2, tiled=True)
    attended = merged.reshape(1, local_rows, QH * HD)
    return (attended, cache_keys, cache_values)


def solution(mesh):
    in_specs = (
        P(("groups", "handoff"), ("blk", "ulysses"), None),
        P(("groups", "handoff"), ("blk", "ulysses"), None),
        P(("groups", "handoff"), ("blk", "ulysses"), None),
        P("groups", None),
        P("groups", None),
    )
    out_specs = (
        P(("groups", "handoff"), ("blk", "ulysses"), None),
        P(("groups", "blk", "handoff"), "ulysses", None, None),
        P(("groups", "blk", "handoff"), "ulysses", None, None),
    )
    return jax.shard_map(body, mesh=mesh, in_specs=in_specs, out_specs=out_specs, check_vma=False)
```

profile of v0, /device:TPU:0, one launch (start us, length us, event | category | flops | bytes accessed | tf_op | source)
XLA Modules:
  0.0 139.1 jit_solution(2987431555794553390)
XLA Ops:
  0.6 1.1 reshape_squeeze.9
  1.8 0.7 copy.73
  2.5 6.3 %all-to-all-start = ((bf16[64,4,512]{2,0,1:T(8,128)(2,1)}), bf16[64,4,512]{2,0,1:T(8,128)(2,1)S(1)}, u32[]{:S(2)}, u32[]{:S(2)}) async-start(bf16[64,4,512]{2,0,1:T(8,128)(2,1)} %copy.73), calls=%async_computation | async-start | bytes 524288 | tf_op jit(solution)/shard_map/all_to_all | solution.py:72
  8.9 0.7 fusion.31
  9.7 0.7 fusion.30
  10.5 0.8 reshape.241
  11.2 0.8 dynamic-slice_bitcast_fusion
  12.0 0.7 sort.46
  12.8 1.1 reshape_squeeze.10
  14.0 0.7 copy.74
  14.8 2.9 %all-to-all-done = bf16[64,4,512]{2,0,1:T(8,128)(2,1)S(1)} async-done(((bf16[64,4,512]{2,0,1:T(8,128)(2,1)}), bf16[64,4,512]{2,0,1:T(8,128)(2,1)S(1)}, u32[]{:S(2)}, u32[]{:S(2)}) %all-to-all-start) | async-done | bytes 262176 | tf_op jit(solution)/shard_map/all_to_all | solution.py:72
  17.8 3.4 %all-to-all-start.1 = ((bf16[64,4,512]{2,0,1:T(8,128)(2,1)}), bf16[64,4,512]{2,0,1:T(8,128)(2,1)S(1)}, u32[]{:S(2)}, u32[]{:S(2)}) async-start(bf16[64,4,512]{2,0,1:T(8,128)(2,1)} %copy.74), calls=%async_computation.1 | async-start | bytes 524288 | tf_op jit(solution)/shard_map/all_to_all | solution.py:73
  21.2 1.4 %reshape_squeeze.11 = bf16[64,4,1024]{2,1,0:T(4,128)(2,1)S(1)} reshape(bf16[1,64,4096]{2,1,0:T(8,128)(2,1)} %param.7) | data formatting | bytes 1048576 | tf_op jit(solution)/shard_map/reshape;squeeze | solution.py:64
  22.7 1.0 copy.77
  23.6 0.6 sort.47
  24.4 0.5 multiply_cosine_fusion
  24.9 3.3 %all-to-all-done.1 = bf16[64,4,512]{2,0,1:T(8,128)(2,1)S(1)} async-done(((bf16[64,4,512]{2,0,1:T(8,128)(2,1)}), bf16[64,4,512]{2,0,1:T(8,128)(2,1)S(1)}, u32[]{:S(2)}, u32[]{:S(2)}) %all-to-all-start.1) | async-done | bytes 262176 | tf_op jit(solution)/shard_map/all_to_all | solution.py:73
  28.2 3.5 %all-to-all-start.2 = ((bf16[64,4,1024]{2,0,1:T(8,128)(2,1)}), bf16[64,4,1024]{2,0,1:T(8,128)(2,1)S(1)}, u32[]{:S(2)}, u32[]{:S(2)}) async-start(bf16[64,4,1024]{2,0,1:T(8,128)(2,1)} %copy.77), calls=%async_computation.2 | async-start | bytes 1048576 | tf_op jit(solution)/shard_map/all_to_all | solution.py:71
  31.9 0.5 multiply_subtract_fusion
  32.4 0.4 maximum_convert_fusion
  33.2 4.2 %collective-permute-start = (bf16[2,256,512]{2,1,0:T(8,128)(2,1)S(1)}, bf16[2,256,512]{2,1,0:T(8,128)(2,1)}, u32[]{:S(2)}, u32[]{:S(2)}) collective-permute-start(bf16[2,256,512]{2,1,0:T(8,128)(2,1)S(1)} %pad_maximum_fusion.1), channel_id=1, source_target_pairs={{0,2},{1,3},{4,6},{5,7},{8,10},{9,11},{12,14},{13,15},{16,18},{17,... | collective-permute-start | bytes 1572872 | tf_op jit(solution)/shard_map/ppermute | solution.py:23
  37.6 1.4 %gather_fusion = bf16[4,2,64,4,128]{4,2,3,1,0:T(8,128)(2,1)} fusion(bf16[2,4,64,4,128]{4,2,3,1,0:T(8,128)(2,1)S(1)} %pad_maximum_fusion.3, s32[1024]{0:T(1024)S(1)} %pad_clamp_fusion.1), kind=kCustom, calls=%fused_computation | custom fusion | bytes 1048592 | tf_op jit(solution)/shard_map/gather | solution.py:93
  39.0 4.4 %all-to-all-done.2 = bf16[64,4,1024]{2,0,1:T(8,128)(2,1)S(1)} async-done(((bf16[64,4,1024]{2,0,1:T(8,128)(2,1)}), bf16[64,4,1024]{2,0,1:T(8,128)(2,1)S(1)}, u32[]{:S(2)}, u32[]{:S(2)}) %all-to-all-start.2) | async-done | bytes 524320 | tf_op jit(solution)/shard_map/all_to_all | solution.py:71
  43.4 3.5 %all-to-all-start.4 = ((bf16[2,4,1,4,64,128]{5,4,3,0,2,1:T(8,128)(2,1)}), bf16[2,4,1,4,64,128]{5,4,3,0,2,1:T(8,128)(2,1)S(1)}, u32[]{:S(2)}, u32[]{:S(2)}) async-start(bf16[2,4,1,4,64,128]{5,4,3,0,2,1:T(8,128)(2,1)} %bitcast.30), calls=%async_computation.4 | async-start | bytes 1048576 | tf_op jit(solution)/shard_map/all_to_all | solution.py:96
  47.2 0.5 subtract_convert_fusion
  47.9 0.3 pad_maximum_fusion.2
  48.2 1.2 copy.75
  49.4 5.6 %pad_maximum_fusion = bf16[2,4352,512]{1,2,0:T(8,128)(2,1)} fusion(bf16[2,256,512]{1,2,0:T(8,128)(2,1)S(1)} %copy.76, bf16[2,256,512]{1,2,0:T(8,128)(2,1)S(1)} %copy.75, bf16[4352]{0:T(1024)(128)(2,1)S(1)} %pad.4.clone), kind=kLoop, calls=%fused_computation.27 | loop fusion | flops 26738688 | bytes 9970176 | tf_op jit(solution)/shard_map/concatenate | solution.py:114
  55.0 62.5 %while.12 = (s32[]{:T(128)}, bf16[2,128,4,2,128]{4,3,2,1,0:T(2,128)(2,1)S(1)}, s32[2]{0:T(128)S(1)}, bf16[2,4352,512]{1,2,0:T(8,128)(2,1)}, s32[256]{0:T(256)S(1...) while((s32[]{:T(128)}, ...), condition=%wide.region_6.7_spmd, body=%wide.region_4.6_spmd.sunk | while | flops 2253245440 | bytes 63871488 | solution.py:154
  55.0 0.6 dynamic_slice.76
  59.2 0.8 fusion.43
  59.9 7.8 %constant_dynamic-slice_fusion.4 = (bf16[1,4224,512]{1,2,0:T(8,128)(2,1)S(1)}, bf16[1,4224,512]{1,2,0:T(8,128)(2,1)S(1)}) fusion(bf16[2,4352,512]{1,2,0:T(8,128)(2,1)} %get-tuple-element.256, s32[]{:T(128)S(6)} %select_n.94, s32[]{:T(128)S(6)} %add.104), kind=kLoop, calls=%fused_computation.23.clone.1 | loop fusion | bytes 17301512 | tf_op jit(solution)/shard_map/while/body/eval_jaxpr/slice | solution.py:125
  67.7 9.2 %fusion.44 = (f32[4,128,2]{1,2,0:T(2,128)S(1)}, f32[4,128,2,4224]{3,1,2,0:T(8,128)}) fusion(pred[128,4224]{1,0:T(8,128)(4,1)S(1)} %fusion.43, bf16[4224,4,128,1]{0,2,3,1:T(8,128)(2,1)S(1)} %bitcast.106, bf16[256,4,2,128]{3,0,2,1:T(8,128)(2,1)S(1)} %get-tuple-element.261, s32[]{:T(128)S(6)} %select_n.95), kind=kOutput, calls=%fused_computation.4.clone.1 | convolution fusion | flops 1124596736 | bytes 22433796 | tf_op jit(solution)/shard_map/while/body/eval_jaxpr/qgrd,kgd->gqrk/dot_general | solution.py:128
  76.9 8.9 %fusion.45 = bf16[1,128,4,2,128]{1,4,3,2,0:T(8,128)(2,1)S(1)} fusion(bf16[4224,4,128,1]{0,2,3,1:T(8,128)(2,1)S(1)} %bitcast.105, f32[4,128,2,4224]{3,1,2,0:T(8,128)} %get-tuple-element.223, pred[128,4224]{1,0:T(8,128)(4,1)S(1)} %fusion.43, f32[128,4,2]{0,2,1:T(2,128)S(1)} %bitcast.117), kind=kOutput, calls=%fused_computation.16.clone.1 | convolution fusion | flops 1124859904 | bytes 22433792 | tf_op jit(solution)/shard_map/while/body/eval_jaxpr/gqrk,kgd->qgrd/dot_general | solution.py:145
  86.1 0.2 constant_dynamic-update-slice_fusion.2
  86.3 0.6 dynamic_slice.76
  90.4 0.8 fusion.43
  91.2 7.7 %constant_dynamic-slice_fusion.4 = (bf16[1,4224,512]{1,2,0:T(8,128)(2,1)S(1)}, bf16[1,4224,512]{1,2,0:T(8,128)(2,1)S(1)}) fusion(bf16[2,4352,512]{1,2,0:T(8,128)(2,1)} %get-tuple-element.256, s32[]{:T(128)S(6)} %select_n.94, s32[]{:T(128)S(6)} %add.104), kind=kLoop, calls=%fused_computation.23.clone.1 | loop fusion | bytes 17301512 | tf_op jit(solution)/shard_map/while/body/eval_jaxpr/slice | solution.py:125
  98.9 9.2 %fusion.44 = (f32[4,128,2]{1,2,0:T(2,128)S(1)}, f32[4,128,2,4224]{3,1,2,0:T(8,128)}) fusion(pred[128,4224]{1,0:T(8,128)(4,1)S(1)} %fusion.43, bf16[4224,4,128,1]{0,2,3,1:T(8,128)(2,1)S(1)} %bitcast.106, bf16[256,4,2,128]{3,0,2,1:T(8,128)(2,1)S(1)} %get-tuple-element.261, s32[]{:T(128)S(6)} %select_n.95), kind=kOutput, calls=%fused_computation.4.clone.1 | convolution fusion | flops 1124596736 | bytes 22433796 | tf_op jit(solution)/shard_map/while/body/eval_jaxpr/qgrd,kgd->gqrk/dot_general | solution.py:128
  108.1 8.9 %fusion.45 = bf16[1,128,4,2,128]{1,4,3,2,0:T(8,128)(2,1)S(1)} fusion(bf16[4224,4,128,1]{0,2,3,1:T(8,128)(2,1)S(1)} %bitcast.105, f32[4,128,2,4224]{3,1,2,0:T(8,128)} %get-tuple-element.223, pred[128,4224]{1,0:T(8,128)(4,1)S(1)} %fusion.43, f32[128,4,2]{0,2,1:T(2,128)S(1)} %bitcast.117), kind=kOutput, calls=%fused_computation.16.clone.1 | convolution fusion | flops 1124859904 | bytes 22433792 | tf_op jit(solution)/shard_map/while/body/eval_jaxpr/gqrk,kgd->qgrd/dot_general | solution.py:145
  117.5 1.2 reshape.238
  118.7 3.5 %all-to-all-start.3 = ((bf16[4,64,1,1024]{3,1,2,0:T(8,128)(2,1)}), bf16[4,64,1,1024]{3,1,2,0:T(8,128)(2,1)S(1)}, u32[]{:S(2)}, u32[]{:S(2)}) async-start(bf16[4,64,1,1024]{3,1,2,0:T(8,128)(2,1)} %bitcast.22), calls=%async_computation.3 | async-start | bytes 1048576 | tf_op jit(solution)/shard_map/all_to_all | solution.py:156
  122.2 0.7 sort.48
  123.0 1.3 gather_fusion.2
  124.2 1.3 gather_fusion.1
  125.5 12.0 %all-to-all-done.3 = bf16[4,64,1,1024]{3,1,2,0:T(8,128)(2,1)S(1)} async-done(((bf16[4,64,1,1024]{3,1,2,0:T(8,128)(2,1)}), bf16[4,64,1,1024]{3,1,2,0:T(8,128)(2,1)S(1)}, u32[]{:S(2)}, u32[]{:S(2)}) %all-to-all-start.3) | async-done | bytes 524320 | tf_op jit(solution)/shard_map/all_to_all | solution.py:156
  137.5 0.4 copy.82
  137.9 1.2 reshape.239
  (50 shorter events, 3.1 us)
Async XLA Ops:
  2.5 15.3 %all-to-all-start = ((bf16[64,4,512]{2,0,1:T(8,128)(2,1)}), bf16[64,4,512]{2,0,1:T(8,128)(2,1)S(1)}, u32[]{:S(2)}, u32[]{:S(2)}) async-start(bf16[64,4,512]{2,0,1:T(8,128)(2,1)} %copy.73), calls=%async_computation | async-start | bytes 524288 | tf_op jit(solution)/shard_map/all_to_all | solution.py:72
  17.8 10.4 %all-to-all-start.1 = ((bf16[64,4,512]{2,0,1:T(8,128)(2,1)}), bf16[64,4,512]{2,0,1:T(8,128)(2,1)S(1)}, u32[]{:S(2)}, u32[]{:S(2)}) async-start(bf16[64,4,512]{2,0,1:T(8,128)(2,1)} %copy.74), calls=%async_computation.1 | async-start | bytes 524288 | tf_op jit(solution)/shard_map/all_to_all | solution.py:73
  28.2 15.2 %all-to-all-start.2 = ((bf16[64,4,1024]{2,0,1:T(8,128)(2,1)}), bf16[64,4,1024]{2,0,1:T(8,128)(2,1)S(1)}, u32[]{:S(2)}, u32[]{:S(2)}) async-start(bf16[64,4,1024]{2,0,1:T(8,128)(2,1)} %copy.77), calls=%async_computation.2 | async-start | bytes 1048576 | tf_op jit(solution)/shard_map/all_to_all | solution.py:71
  33.2 15.0 %collective-permute-start = (bf16[2,256,512]{2,1,0:T(8,128)(2,1)S(1)}, bf16[2,256,512]{2,1,0:T(8,128)(2,1)}, u32[]{:S(2)}, u32[]{:S(2)}) collective-permute-start(bf16[2,256,512]{2,1,0:T(8,128)(2,1)S(1)} %pad_maximum_fusion.1), channel_id=1, source_target_pairs={{0,2},{1,3},{4,6},{5,7},{8,10},{9,11},{12,14},{13,15},{16,18},{17,... | collective-permute-start | bytes 1572872 | tf_op jit(solution)/shard_map/ppermute | solution.py:23
  43.4 75.3 %all-to-all-start.4 = ((bf16[2,4,1,4,64,128]{5,4,3,0,2,1:T(8,128)(2,1)}), bf16[2,4,1,4,64,128]{5,4,3,0,2,1:T(8,128)(2,1)S(1)}, u32[]{:S(2)}, u32[]{:S(2)}) async-start(bf16[2,4,1,4,64,128]{5,4,3,0,2,1:T(8,128)(2,1)} %bitcast.30), calls=%async_computation.4 | async-start | bytes 1048576 | tf_op jit(solution)/shard_map/all_to_all | solution.py:96
  118.7 18.8 %all-to-all-start.3 = ((bf16[4,64,1,1024]{3,1,2,0:T(8,128)(2,1)}), bf16[4,64,1,1024]{3,1,2,0:T(8,128)(2,1)S(1)}, u32[]{:S(2)}, u32[]{:S(2)}) async-start(bf16[4,64,1,1024]{3,1,2,0:T(8,128)(2,1)} %bitcast.22), calls=%async_computation.3 | async-start | bytes 1048576 | tf_op jit(solution)/shard_map/all_to_all | solution.py:156
where the time goes:
time: 140 us; the launch traced here: 139 us
  matrix products  36.3 us (26%)
  local copies, waits for them, and re-layouts  35.3 us (25%)
  starting transfers between devices  24.4 us (17%)
  waiting for transfers between devices  22.6 us (16%)
  other arithmetic  13 us (9%)
  loops' own time  6.54 us (5%)
    dot_general x2, matrix products, attend(): jnp.einsum('qgrd,kgd->gqrk', query_block, key_block, preferred_element_ty...  18.5 us
    dot_general x2, matrix products, attend(): jnp.einsum('gqrk,kgd->qgrd', weights.astype(jnp.bfloat16), value_block, p...  17.8 us
    slice x2, local copies, waits for them, and re-layouts, attend(): key_block = kv_block[0].reshape(key_span, kv_local, HD)  15.5 us
    all_to_all x1, waiting for transfers between devices, body(): lax.all_to_all(outgoing_heads, 'ulysses', split_axis=0, concat_axis=2, ti...  12 us
    another operation x1, loops' own time, body(): blocks = lax.map(attend, starts)  6.54 us
    all_to_all x1, starting transfers between devices, body(): lax.all_to_all(key_split, 'ulysses', split_axis=1, concat_axis=0, tiled=T...  6.35 us
    concatenate x1, other arithmetic, body(): jnp.concatenate([front_zeros] + earlier[::-1] + [local_kv], axis=1)  5.59 us
    all_to_all x1, waiting for transfers between devices, body(): lax.all_to_all(query_split, 'ulysses', split_axis=1, concat_axis=0, tiled...  4.37 us
  transfers between devices with their start and end apart: 6, of which 4 were waited for; matrix products, arithmetic and copies ran while one was open for 58% of the time, Pallas kernels for 0%

commit v1 on v0

--- a/solution.py
+++ b/solution.py
@@ -57,7 +57,7 @@
     pack_index = lax.axis_index("handoff")
     blk_index = lax.axis_index("blk")
     shard_rows = local_rows * ulysses_size
-    window = WINDOW
+    window = min(WINDOW, page_table.shape[1] // 2 * PAGE)
     earlier_count = min(window // shard_rows, blk_size - 1)
     kv_local = KVH // ulysses_size
     group_size = QH // KVH

time: 140 us -> 88.3 us (0.63)
  matrix products: 36.3 us -> 2.22 us
  local copies, waits for them, and re-layouts: 35.3 us -> 19.2 us
  other arithmetic: 13 us -> 6.52 us
  waiting for transfers between devices: 22.6 us -> 27.5 us
    dot_general x2, matrix products: 17.8 us -> 0.76 us  [attend(): jnp.einsum('gqrk,kgd->qgrd', weights.astype(jnp.bfloat16), value_block, p...]
    dot_general x2, matrix products: 18.5 us -> 1.45 us  [attend(): jnp.einsum('qgrd,kgd->gqrk', query_block, key_block, preferred_element_ty...]
    slice x2, local copies, waits for them, and re-layouts: 15.5 us -> 0.39 us  [attend(): key_block = kv_block[0].reshape(key_span, kv_local, HD)]
    concatenate x1, other arithmetic: 5.59 us -> 1.11 us  [body(): jnp.concatenate([front_zeros] + earlier[::-1] + [local_kv], axis=1)]
    all_to_all x1, waiting for transfers between devices: 2.94 us -> 6.59 us  [body(): lax.all_to_all(key_split, 'ulysses', split_axis=1, concat_axis=0, tiled=T...]
    while x0 -> x12, local copies, waits for them, and re-layouts: none -> 3.35 us
  transfers between devices with their start and end apart: 6 -> 6, of which waited for: 4 -> 4; matrix products, arithmetic and copies ran while one was open for 58% -> 25% of each run, Pallas kernels for 0% -> 0%
where the time goes in v1:
time: 88.3 us; the launch traced here: 87.5 us
  waiting for transfers between devices  27.5 us (31%)
  starting transfers between devices  24.5 us (28%)
  local copies, waits for them, and re-layouts  19.2 us (22%)
  loops' own time  6.61 us (7%)
  other arithmetic  6.52 us (7%)
  matrix products  2.22 us (3%)
  between operations  0.94 us (1%)
    all_to_all x1, waiting for transfers between devices, body(): lax.all_to_all(outgoing_heads, 'ulysses', split_axis=0, concat_axis=2, ti...  12 us
    another operation x1, loops' own time, body(): blocks = lax.map(attend, starts)  6.61 us
    all_to_all x1, waiting for transfers between devices, body(): lax.all_to_all(key_split, 'ulysses', split_axis=1, concat_axis=0, tiled=T...  6.59 us
    all_to_all x1, starting transfers between devices, body(): lax.all_to_all(key_split, 'ulysses', split_axis=1, concat_axis=0, tiled=T...  6.48 us
    all_to_all x1, waiting for transfers between devices, body(): lax.all_to_all(query_split, 'ulysses', split_axis=1, concat_axis=0, tiled...  4.61 us
    all_to_all x1, waiting for transfers between devices, body(): lax.all_to_all(value_split, 'ulysses', split_axis=1, concat_axis=0, tiled...  4.36 us
    ppermute x1, starting transfers between devices, from_behind(): return lax.ppermute(block, axis, route)  4.21 us
    all_to_all x1, starting transfers between devices, body(): lax.all_to_all(outgoing_heads, 'ulysses', split_axis=0, concat_axis=2, ti...  3.47 us
  transfers between devices with their start and end apart: 6, of which 4 were waited for; matrix products, arithmetic and copies ran while one was open for 25% of the time, Pallas kernels for 0%

profile of v1, /device:TPU:0, one launch (start us, length us, event | category | flops | bytes accessed | tf_op | source)
XLA Modules:
  0.0 87.5 jit_solution(2109109784763567030)
XLA Ops:
  0.7 1.2 %reshape_squeeze.9 = bf16[64,4,512]{2,1,0:T(4,128)(2,1)S(1)} reshape(bf16[1,64,2048]{2,1,0:T(8,128)(2,1)} %param.8) | data formatting | bytes 524288 | tf_op jit(solution)/shard_map/reshape;squeeze | solution.py:65
  1.8 0.7 copy.70
  2.6 6.5 %all-to-all-start = ((bf16[64,4,512]{2,0,1:T(8,128)(2,1)}), bf16[64,4,512]{2,0,1:T(8,128)(2,1)S(1)}, u32[]{:S(2)}, u32[]{:S(2)}) async-start(bf16[64,4,512]{2,0,1:T(8,128)(2,1)} %copy.70), calls=%async_computation | async-start | bytes 524288 | tf_op jit(solution)/shard_map/all_to_all | solution.py:72
  9.5 0.7 sort.46
  10.5 0.7 copy.71
  11.4 6.6 %all-to-all-done = bf16[64,4,512]{2,0,1:T(8,128)(2,1)S(1)} async-done(((bf16[64,4,512]{2,0,1:T(8,128)(2,1)}), bf16[64,4,512]{2,0,1:T(8,128)(2,1)S(1)}, u32[]{:S(2)}, u32[]{:S(2)}) %all-to-all-start) | async-done | bytes 262176 | tf_op jit(solution)/shard_map/all_to_all | solution.py:72
  18.0 3.4 %all-to-all-start.1 = ((bf16[64,4,512]{2,0,1:T(8,128)(2,1)}), bf16[64,4,512]{2,0,1:T(8,128)(2,1)S(1)}, u32[]{:S(2)}, u32[]{:S(2)}) async-start(bf16[64,4,512]{2,0,1:T(8,128)(2,1)} %copy.71), calls=%async_computation.1 | async-start | bytes 524288 | tf_op jit(solution)/shard_map/all_to_all | solution.py:73
  21.4 0.4 reshape_squeeze.11
  21.8 1.0 %copy.72 = bf16[64,4,1024]{2,0,1:T(8,128)(2,1)} copy(bf16[64,4,1024]{2,1,0:T(4,128)(2,1)S(1)} %reshape_squeeze.11) | data formatting | bytes 1048576 | tf_op jit(solution)/shard_map/reshape;squeeze | solution.py:64
  22.8 0.6 sort.47
  23.5 0.5 multiply_cosine_fusion
  24.0 4.4 %all-to-all-done.1 = bf16[64,4,512]{2,0,1:T(8,128)(2,1)S(1)} async-done(((bf16[64,4,512]{2,0,1:T(8,128)(2,1)}), bf16[64,4,512]{2,0,1:T(8,128)(2,1)S(1)}, u32[]{:S(2)}, u32[]{:S(2)}) %all-to-all-start.1) | async-done | bytes 262176 | tf_op jit(solution)/shard_map/all_to_all | solution.py:73
  28.4 3.5 %all-to-all-start.2 = ((bf16[64,4,1024]{2,0,1:T(8,128)(2,1)}), bf16[64,4,1024]{2,0,1:T(8,128)(2,1)S(1)}, u32[]{:S(2)}, u32[]{:S(2)}) async-start(bf16[64,4,1024]{2,0,1:T(8,128)(2,1)} %copy.72), calls=%async_computation.2 | async-start | bytes 1048576 | tf_op jit(solution)/shard_map/all_to_all | solution.py:71
  32.1 0.5 multiply_subtract_fusion
  32.6 0.4 maximum_convert_fusion
  33.3 4.2 %collective-permute-start = (bf16[2,256,512]{2,1,0:T(8,128)(2,1)S(1)}, bf16[2,256,512]{2,1,0:T(8,128)(2,1)}, u32[]{:S(2)}, u32[]{:S(2)}) collective-permute-start(bf16[2,256,512]{2,1,0:T(8,128)(2,1)S(1)} %pad_maximum_fusion), channel_id=1, source_target_pairs={{0,2},{1,3},{4,6},{5,7},{8,10},{9,11},{12,14},{13,15},{16,18},{17,... | collective-permute-start | bytes 1572872 | tf_op jit(solution)/shard_map/ppermute | solution.py:23
  37.6 1.4 %gather_fusion = bf16[4,2,64,4,128]{4,2,3,1,0:T(8,128)(2,1)} fusion(bf16[2,4,64,4,128]{4,2,3,1,0:T(8,128)(2,1)S(1)} %pad_maximum_fusion.2, s32[1024]{0:T(1024)S(1)} %pad_clamp_fusion.1), kind=kCustom, calls=%fused_computation | custom fusion | bytes 1048592 | tf_op jit(solution)/shard_map/gather | solution.py:93
  39.0 4.6 %all-to-all-done.2 = bf16[64,4,1024]{2,0,1:T(8,128)(2,1)S(1)} async-done(((bf16[64,4,1024]{2,0,1:T(8,128)(2,1)}), bf16[64,4,1024]{2,0,1:T(8,128)(2,1)S(1)}, u32[]{:S(2)}, u32[]{:S(2)}) %all-to-all-start.2) | async-done | bytes 524320 | tf_op jit(solution)/shard_map/all_to_all | solution.py:71
  43.6 3.5 %all-to-all-start.4 = ((bf16[2,4,1,4,64,128]{5,4,3,0,2,1:T(8,128)(2,1)}), bf16[2,4,1,4,64,128]{5,4,3,0,2,1:T(8,128)(2,1)S(1)}, u32[]{:S(2)}, u32[]{:S(2)}) async-start(bf16[2,4,1,4,64,128]{5,4,3,0,2,1:T(8,128)(2,1)} %bitcast.30), calls=%async_computation.4 | async-start | bytes 1048576 | tf_op jit(solution)/shard_map/all_to_all | solution.py:96
  47.2 0.2 copy.104
  47.4 0.5 subtract_convert_fusion
  48.1 0.3 pad_maximum_fusion.1
  48.4 1.1 %maximum_maximum_fusion = bf16[2,512,512]{2,1,0:T(8,128)(2,1)S(1)} fusion(bf16[1,256,512]{2,1,0:T(8,128)(2,1)S(1)} %bitcast.114, bf16[1,256,512]{2,1,0:T(8,128)(2,1)S(1)} %convert_element_type.81, bf16[2,256,512]{2,1,0:T(8,128)(2,1)} %collective-permute-done), kind=kLoop, calls=%fused_computation.20 | loop fusion | flops 3145728 | bytes 2097152 | tf_op jit(solution)/shard_map/concatenate | solution.py:114
  49.5 15.4 %while.12 = (s32[]{:T(128)}, bf16[2,128,4,2,128]{4,3,2,1,0:T(2,128)(2,1)}, s32[2]{0:T(128)S(1)}, bf16[2,512,512]{2,1,0:T(8,128)(2,1)S(1)}, s32[256]{0:T(256)S(1)...) while((s32[]{:T(128)}, ...), condition=%wide.region_6.7_spmd, body=%wide.region_4.6_spmd.sunk | while | flops 203898240 | bytes 11392056 | solution.py:154
  49.5 0.6 dynamic_slice.76
  54.0 0.2 copy.108
  54.2 0.2 copy.109
  54.4 0.7 fusion.29
  55.1 0.4 fusion.30
  55.7 0.5 copy-done.1
  56.2 0.2 constant_dynamic-update-slice_fusion.2
  56.4 0.8 copy-done.2
  57.2 0.6 dynamic_slice.76
  61.6 0.2 copy.108
  61.9 0.2 copy.109
  62.1 0.7 fusion.29
  62.8 0.4 fusion.30
  63.4 0.5 copy-done.1
  63.9 0.2 constant_dynamic-update-slice_fusion.2
  64.1 0.8 copy-done.2
  64.9 2.2 %reshape.238 = bf16[4,64,1,1024]{3,1,0,2:T(8,128)(2,1)} reshape(bf16[2,128,4,2,128]{4,3,2,1,0:T(2,128)(2,1)} %get-tuple-element.120) | data formatting | bytes 1048576 | tf_op jit(solution)/shard_map/reshape | solution.py:155
  67.1 3.5 %all-to-all-start.3 = ((bf16[4,64,1,1024]{3,1,2,0:T(8,128)(2,1)}), bf16[4,64,1,1024]{3,1,2,0:T(8,128)(2,1)S(1)}, u32[]{:S(2)}, u32[]{:S(2)}) async-start(bf16[4,64,1,1024]{3,1,2,0:T(8,128)(2,1)} %bitcast.22), calls=%async_computation.3 | async-start | bytes 1048576 | tf_op jit(solution)/shard_map/all_to_all | solution.py:156
  70.6 0.7 sort.48
  71.4 1.3 %gather_fusion.2 = bf16[4,4,64,128]{3,2,1,0:T(8,128)(2,1)} fusion(bf16[4,4,64,128]{3,2,1,0:T(8,128)(2,1)S(1)} %get-tuple-element.190, s32[1024]{0:T(1024)S(1)} %pad_clamp_fusion), kind=kCustom, calls=%fused_computation.2 | custom fusion | bytes 524304 | tf_op jit(solution)/shard_map/gather | solution.py:109
  72.7 1.3 %gather_fusion.1 = bf16[4,4,64,128]{3,2,1,0:T(8,128)(2,1)} fusion(bf16[4,4,64,128]{3,2,1,0:T(8,128)(2,1)S(1)} %get-tuple-element.191, s32[1024]{0:T(1024)S(1)} %pad_clamp_fusion), kind=kCustom, calls=%fused_computation.1 | custom fusion | bytes 524304 | tf_op jit(solution)/shard_map/gather | solution.py:108
  73.9 12.0 %all-to-all-done.3 = bf16[4,64,1,1024]{3,1,2,0:T(8,128)(2,1)S(1)} async-done(((bf16[4,64,1,1024]{3,1,2,0:T(8,128)(2,1)}), bf16[4,64,1,1024]{3,1,2,0:T(8,128)(2,1)S(1)}, u32[]{:S(2)}, u32[]{:S(2)}) %all-to-all-start.3) | async-done | bytes 524320 | tf_op jit(solution)/shard_map/all_to_all | solution.py:156
  85.9 0.4 copy.78
  86.3 1.2 %reshape.239 = bf16[1,64,4096]{2,1,0:T(8,128)(2,1)} reshape(bf16[1,64,4,1,1024]{4,2,1,3,0:T(4,128)(2,1)S(1)} %copy.78) | data formatting | bytes 1048576 | tf_op jit(solution)/shard_map/reshape | solution.py:157
  (66 shorter events, 3.4 us)
Async XLA Ops:
  0.6 8.4 %copy-start.5 = (s32[2,4]{1,0:T(2,128)S(1)}, s32[2,4]{1,0:T(2,128)}, u32[]{:S(2)}) copy-start(s32[2,4]{1,0:T(2,128)} %param.10) | copy-start | bytes 100
  0.6 8.7 %copy-start.4 = (s32[2,8]{1,0:T(2,128)S(1)}, s32[2,8]{1,0:T(2,128)}, u32[]{:S(2)}) copy-start(s32[2,8]{1,0:T(2,128)} %param.11) | copy-start | bytes 196
  0.7 9.7 %copy-start.3 = (bf16[1,64,2048]{2,1,0:T(8,128)(2,1)S(1)}, bf16[1,64,2048]{2,1,0:T(8,128)(2,1)}, u32[]{:S(2)}) copy-start(bf16[1,64,2048]{2,1,0:T(8,128)(2,1)} %param.9) | copy-start | bytes 786436
  2.6 18.8 %copy-start = (bf16[1,64,4096]{2,1,0:T(8,128)(2,1)S(1)}, bf16[1,64,4096]{2,1,0:T(8,128)(2,1)}, u32[]{:S(2)}) copy-start(bf16[1,64,4096]{2,1,0:T(8,128)(2,1)} %param.7) | copy-start | bytes 1572868
  2.6 15.4 %all-to-all-start = ((bf16[64,4,512]{2,0,1:T(8,128)(2,1)}), bf16[64,4,512]{2,0,1:T(8,128)(2,1)S(1)}, u32[]{:S(2)}, u32[]{:S(2)}) async-start(bf16[64,4,512]{2,0,1:T(8,128)(2,1)} %copy.70), calls=%async_computation | async-start | bytes 524288 | tf_op jit(solution)/shard_map/all_to_all | solution.py:72
  18.0 10.4 %all-to-all-start.1 = ((bf16[64,4,512]{2,0,1:T(8,128)(2,1)}), bf16[64,4,512]{2,0,1:T(8,128)(2,1)S(1)}, u32[]{:S(2)}, u32[]{:S(2)}) async-start(bf16[64,4,512]{2,0,1:T(8,128)(2,1)} %copy.71), calls=%async_computation.1 | async-start | bytes 524288 | tf_op jit(solution)/shard_map/all_to_all | solution.py:73
  28.4 15.2 %all-to-all-start.2 = ((bf16[64,4,1024]{2,0,1:T(8,128)(2,1)}), bf16[64,4,1024]{2,0,1:T(8,128)(2,1)S(1)}, u32[]{:S(2)}, u32[]{:S(2)}) async-start(bf16[64,4,1024]{2,0,1:T(8,128)(2,1)} %copy.72), calls=%async_computation.2 | async-start | bytes 1048576 | tf_op jit(solution)/shard_map/all_to_all | solution.py:71
  33.3 15.0 %collective-permute-start = (bf16[2,256,512]{2,1,0:T(8,128)(2,1)S(1)}, bf16[2,256,512]{2,1,0:T(8,128)(2,1)}, u32[]{:S(2)}, u32[]{:S(2)}) collective-permute-start(bf16[2,256,512]{2,1,0:T(8,128)(2,1)S(1)} %pad_maximum_fusion), channel_id=1, source_target_pairs={{0,2},{1,3},{4,6},{5,7},{8,10},{9,11},{12,14},{13,15},{16,18},{17,... | collective-permute-start | bytes 1572872 | tf_op jit(solution)/shard_map/ppermute | solution.py:23
  43.6 23.5 %all-to-all-start.4 = ((bf16[2,4,1,4,64,128]{5,4,3,0,2,1:T(8,128)(2,1)}), bf16[2,4,1,4,64,128]{5,4,3,0,2,1:T(8,128)(2,1)S(1)}, u32[]{:S(2)}, u32[]{:S(2)}) async-start(bf16[2,4,1,4,64,128]{5,4,3,0,2,1:T(8,128)(2,1)} %bitcast.30), calls=%async_computation.4 | async-start | bytes 1048576 | tf_op jit(solution)/shard_map/all_to_all | solution.py:96
  55.1 1.0 %copy-start.1 = (bf16[2,128,4,2,128]{4,3,2,1,0:T(2,128)(2,1)S(1)}, bf16[2,128,4,2,128]{4,3,2,1,0:T(2,128)(2,1)}, u32[]{:S(2)}) copy-start(bf16[2,128,4,2,128]{4,3,2,1,0:T(2,128)(2,1)} %get-tuple-element.278) | copy-start | bytes 1572868 | tf_op jit(solution)/shard_map/while
  56.4 0.8 copy-start.2
  62.8 1.0 %copy-start.1 = (bf16[2,128,4,2,128]{4,3,2,1,0:T(2,128)(2,1)S(1)}, bf16[2,128,4,2,128]{4,3,2,1,0:T(2,128)(2,1)}, u32[]{:S(2)}) copy-start(bf16[2,128,4,2,128]{4,3,2,1,0:T(2,128)(2,1)} %get-tuple-element.278) | copy-start | bytes 1572868 | tf_op jit(solution)/shard_map/while
  64.1 0.8 copy-start.2
  67.1 18.8 %all-to-all-start.3 = ((bf16[4,64,1,1024]{3,1,2,0:T(8,128)(2,1)}), bf16[4,64,1,1024]{3,1,2,0:T(8,128)(2,1)S(1)}, u32[]{:S(2)}, u32[]{:S(2)}) async-start(bf16[4,64,1,1024]{3,1,2,0:T(8,128)(2,1)} %bitcast.22), calls=%async_computation.3 | async-start | bytes 1048576 | tf_op jit(solution)/shard_map/all_to_all | solution.py:156

commit v2 on v1

v2 whole, which is shorter than its diff:
```python
import functools

import jax
import jax.numpy as jnp
import numpy as np
from jax import lax
from jax.experimental import pallas as pl
from jax.experimental.pallas import tpu as pltpu
from jax.sharding import PartitionSpec as P

QH = 32
KVH = 16
HD = 128
WINDOW = 4096
PAGE = 64

QUERY_SCALE = 144.0 ** (-0.5)
SOFT_CAP = 50.0
ROPE_BASE = 10000.0
MESH = pl.DeviceIdType.MESH


def turn(x, cosine, sine):
    wide = x.astype(jnp.float32)
    return (wide * cosine + pltpu.roll(wide, HD // 2, 1) * sine).astype(jnp.bfloat16)


def pick(index, choices):
    chosen = choices[0]
    for j in range(1, len(choices)):
        chosen = jnp.where(index == j, choices[j], chosen)
    return chosen


def kernel(
    sizes, q_ref, k_ref, v_ref, freq_ref, pages_ref, table_ref,
    out_ref, ck_ref, cv_ref,
    kraw, tab_k, tab_v, qbuf, obuf, cos_t, sin_t, out_k, out_v, got_k, got_v,
    in_send, in_recv, in_local, x_send, x_recv, c_send, c_recv, c_local, o_send, o_recv, o_local,
):
    ulysses, blks, cores, local, kvl, group, reach, reqs = sizes
    rows = ulysses * local
    slots = rows // PAGE
    sources = blks * cores
    back = min(-(-reach // rows), blks - 1)
    home = back * rows
    qw = group * HD
    me = lax.axis_index("ulysses")
    blk = lax.axis_index("blk")
    pack = lax.axis_index("handoff")
    mine = blk * cores + pack

    barrier = pltpu.get_barrier_semaphore()

    def u_peer(i):
        return lax.rem(me + i, ulysses)

    def s_peer(i):
        p = lax.rem(mine + i, sources)
        return p, {"blk": p // cores, "handoff": lax.rem(p, cores)}

    for i in range(1, ulysses):
        pl.semaphore_signal(barrier, inc=1, device_id={"ulysses": u_peer(i)}, device_id_type=MESH)
    for i in range(1, sources):
        pl.semaphore_signal(barrier, inc=1, device_id=s_peer(i)[1], device_id_type=MESH)

    for hop in range(1, back + 1):
        @pl.when(blk < hop)
        def _():
            part = pl.ds((back - hop) * rows, rows)
            tab_k[:, part, :] = jnp.zeros((kvl, rows, HD), jnp.bfloat16)
            tab_v[:, part, :] = jnp.zeros((kvl, rows, HD), jnp.bfloat16)

    pl.semaphore_wait(barrier, ulysses - 1 + sources - 1)

    def landing(what, h, whose):
        if what == 0:
            return kraw.at[h, pl.ds(whose * local, local), :]
        if what == 1:
            return tab_v.at[h, pl.ds(home + whose * local, local), :]
        return qbuf.at[h, pl.ds(whose * local, local), :]

    def leaving(what, h, whose):
        width = qw if what == 2 else HD
        ref = (k_ref, v_ref, q_ref)[what]
        return ref.at[:, pl.ds(pl.multiple_of((whose * kvl + h) * width, width), width)]

    def incoming(what, h, i):
        return pltpu.make_async_remote_copy(
            src_ref=leaving(what, h, u_peer(i)), dst_ref=landing(what, h, me),
            send_sem=in_send.at[what, h, i - 1], recv_sem=in_recv.at[what, h, i - 1],
            device_id={"ulysses": u_peer(i)}, device_id_type=MESH,
        )

    def own_in(what, h):
        return pltpu.make_async_copy(leaving(what, h, me), landing(what, h, me), in_local.at[what, h])

    order = [(w, h) for h in range(kvl) for w in (0, 1)] + [(2, h) for h in range(kvl)]
    for what, h in order:
        for i in range(1, ulysses):
            incoming(what, h, i).start()
        own_in(what, h).start()

    def arrive(what, h):
        own_in(what, h).wait()
        for i in range(1, ulysses):
            incoming(what, h, i).wait_recv()

    ends = []
    starts = []
    total = jnp.int32(0)
    for r in range(reqs):
        starts.append(total)
        total = total + pages_ref[pack, r] * PAGE
        ends.append(total)

    def first_token(pos):
        first = jnp.zeros_like(pos)
        for r in range(reqs):
            first = jnp.maximum(first, jnp.where(pos >= starts[r], starts[r], 0))
        return first

    pos_rows = blk * rows + lax.broadcasted_iota(jnp.int32, (rows, HD), 0)
    rel = (pos_rows - first_token(pos_rows)).astype(jnp.float32)
    angles = rel * freq_ref[...]
    lanes = lax.broadcasted_iota(jnp.int32, (rows, HD), 1)
    cos_t[...] = jnp.cos(angles)
    sine = jnp.sin(angles)
    sin_t[...] = jnp.where(lanes < HD // 2, -sine, sine)

    def onward(which, h, hop):
        tab = (tab_k, tab_v)[which]
        return pltpu.make_async_remote_copy(
            src_ref=tab.at[h, pl.ds(home, rows), :],
            dst_ref=tab.at[h, pl.ds((back - hop) * rows, rows), :],
            send_sem=x_send.at[which, h, hop - 1], recv_sem=x_recv.at[which, h, hop - 1],
            device_id={"blk": lax.rem(blk + hop, blks)}, device_id_type=MESH,
        )

    for h in range(kvl):
        arrive(0, h)
        tab_k[h, pl.ds(home, rows), :] = turn(kraw[h], cos_t[...], sin_t[...])
        arrive(1, h)
        for hop in range(1, back + 1):
            @pl.when(blk + hop < blks)
            def _():
                onward(0, h, hop).start()
                onward(1, h, hop).start()

    def page_for(owner):
        def step(j, found):
            page = table_ref[pack, blk * slots + j]
            return found + jnp.where(lax.div(page, jnp.int32(slots)) == owner, j, 0)
        return lax.fori_loop(0, slots, step, jnp.int32(0))

    def handed(which, i):
        src, dst = ((out_k, got_k), (out_v, got_v))[which]
        return pltpu.make_async_remote_copy(
            src_ref=src.at[i], dst_ref=dst.at[mine],
            send_sem=c_send.at[which, i - 1], recv_sem=c_recv.at[which, i - 1],
            device_id=s_peer(i)[1], device_id_type=MESH,
        )

    def own_page(which):
        src, dst = ((out_k, got_k), (out_v, got_v))[which]
        return pltpu.make_async_copy(src.at[0], dst.at[mine], c_local.at[which])

    for i in range(sources):
        chosen = page_for(s_peer(i)[0])
        for tab, out in ((tab_k, out_k), (tab_v, out_v)):
            out[i] = pick(chosen, [tab[:, home + j * PAGE:home + (j + 1) * PAGE, :] for j in range(slots)])
    for i in range(1, sources):
        handed(0, i).start()
        handed(1, i).start()
    own_page(0).start()
    own_page(1).start()

    block = min(rows, 128)
    lead = min(-(-reach // block) * block, home)
    span = lead + block
    chunk = span if span <= 512 else block
    factor = QUERY_SCALE / SOFT_CAP

    def attend(h, i):
        at = i * block
        if not isinstance(i, int):
            at = pl.multiple_of(at, block)
        here = pl.ds(at, block)
        cosine, sine_here = cos_t[here, :], sin_t[here, :]
        query = jnp.concatenate(
            [turn(qbuf[h, here, g * HD:(g + 1) * HD], cosine, sine_here) for g in range(group)], axis=0
        )
        pos = blk * rows + at + lax.broadcasted_iota(jnp.int32, (block, 1), 0)
        low = jnp.maximum(first_token(pos), pos - (WINDOW - 1))
        pos = jnp.concatenate([pos] * group, axis=0)
        low = jnp.concatenate([low] * group, axis=0)
        begin = home + at - lead

        def part(c):
            start = begin + c * chunk
            if not isinstance(start, int):
                start = pl.multiple_of(start, block)
            seen = pl.ds(start, chunk)
            scores = lax.dot_general(
                query, tab_k[h, seen, :], (((1,), (1,)), ((), ())), preferred_element_type=jnp.float32
            )
            weights = jnp.exp(SOFT_CAP * jnp.tanh(scores * factor))
            key_pos = (blk - back) * rows + start + lax.broadcasted_iota(jnp.int32, (1, chunk), 1)
            weights = jnp.where((key_pos <= pos) & (key_pos >= low), weights, 0.0)
            total = jnp.sum(weights, axis=1, keepdims=True)
            mixed = jnp.dot(
                weights.astype(jnp.bfloat16), tab_v[h, seen, :], preferred_element_type=jnp.float32
            )
            return mixed, total

        if span == chunk:
            mixed, total = part(0)
        else:
            def step(c, carry):
                mixed, total = part(c)
                return carry[0] + mixed, carry[1] + total
            mixed, total = lax.fori_loop(
                0, span // chunk, step,
                (jnp.zeros((group * block, HD), jnp.float32), jnp.zeros((group * block, 1), jnp.float32)),
            )
        result = (mixed / total).astype(jnp.bfloat16)
        for g in range(group):
            obuf[h, here, g * HD:(g + 1) * HD] = result[g * block:(g + 1) * block]

    def outgoing(h, i):
        return pltpu.make_async_remote_copy(
            src_ref=obuf.at[h, pl.ds(pl.multiple_of(u_peer(i) * local, local), local), :],
            dst_ref=out_ref.at[:, pl.ds(pl.multiple_of((me * kvl + h) * qw, qw), qw)],
            send_sem=o_send.at[h, i - 1], recv_sem=o_recv.at[h, i - 1],
            device_id={"ulysses": u_peer(i)}, device_id_type=MESH,
        )

    def own_out(h):
        return pltpu.make_async_copy(
            obuf.at[h, pl.ds(pl.multiple_of(me * local, local), local), :],
            out_ref.at[:, pl.ds(pl.multiple_of((me * kvl + h) * qw, qw), qw)],
            o_local.at[h],
        )

    for h in range(kvl):
        for hop in range(1, back + 1):
            @pl.when(blk >= hop)
            def _():
                onward(0, h, hop).wait_recv()
                onward(1, h, hop).wait_recv()
        arrive(2, h)
        if rows // block <= 4:
            for i in range(rows // block):
                attend(h, i)
        else:
            def each(i, carry):
                attend(h, i)
                return carry
            lax.fori_loop(0, rows // block, each, 0)
        for i in range(1, ulysses):
            outgoing(h, i).start()
        own_out(h).start()

    own_page(0).wait()
    own_page(1).wait()
    for i in range(1, sources):
        handed(0, i).wait_recv()
        handed(1, i).wait_recv()
    for j in range(slots):
        def step(n, found, j=j):
            s = n // slots
            page = table_ref[lax.rem(s, cores), (s // cores) * slots + lax.rem(n, slots)]
            return found + jnp.where(page == mine * slots + j, s, 0)
        source = lax.fori_loop(0, sources * slots, step, jnp.int32(0))
        ck_ref[j] = pick(source, [got_k[s] for s in range(sources)])
        cv_ref[j] = pick(source, [got_v[s] for s in range(sources)])

    for i in range(1, sources):
        handed(0, i).wait_send()
        handed(1, i).wait_send()
    for what, h in order:
        for i in range(1, ulysses):
            incoming(what, h, i).wait_send()
    for h in range(kvl):
        for hop in range(1, back + 1):
            @pl.when(blk + hop < blks)
            def _():
                onward(0, h, hop).wait_send()
                onward(1, h, hop).wait_send()
    for h in range(kvl):
        own_out(h).wait()
        for i in range(1, ulysses):
            outgoing(h, i).wait()


def body(queries, keys, values, request_pages, page_table):
    local = queries.shape[1]
    ulysses = lax.axis_size("ulysses")
    blks = lax.axis_size("blk")
    cores = lax.axis_size("handoff")
    kvl = KVH // ulysses
    group = QH // KVH
    rows = local * ulysses
    slots = rows // PAGE
    sources = blks * cores
    assert slots == sources
    reach = min(WINDOW, page_table.shape[1] // 2 * PAGE)
    back = min(-(-reach // rows), blks - 1)
    reqs = request_pages.shape[1]
    half = np.arange(HD // 2, dtype=np.float64)
    freq = (ROPE_BASE ** (-2.0 * half / HD)).astype(np.float32)
    freq = jnp.asarray(np.concatenate([freq, freq])[None, :])
    sizes = (ulysses, blks, cores, local, kvl, group, reach, reqs)
    qw = group * HD
    bf = jnp.bfloat16
    dma = pltpu.SemaphoreType.DMA
    hops = max(back, 1)
    anywhere = pl.BlockSpec(memory_space=pl.ANY)
    vmem = pl.BlockSpec(memory_space=pltpu.VMEM)
    smem = pl.BlockSpec(memory_space=pltpu.SMEM)
    attended, cache_keys, cache_values = pl.pallas_call(
        functools.partial(kernel, sizes),
        out_shape=(
            jax.ShapeDtypeStruct((local, QH * HD), bf),
            jax.ShapeDtypeStruct((slots, kvl, PAGE, HD), bf),
            jax.ShapeDtypeStruct((slots, kvl, PAGE, HD), bf),
        ),
        in_specs=[anywhere, anywhere, anywhere, vmem, smem, smem],
        out_specs=(anywhere, vmem, vmem),
        scratch_shapes=[
            pltpu.VMEM((kvl, rows, HD), bf),
            pltpu.VMEM((kvl, (back + 1) * rows, HD), bf),
            pltpu.VMEM((kvl, (back + 1) * rows, HD), bf),
            pltpu.VMEM((kvl, rows, qw), bf),
            pltpu.VMEM((kvl, rows, qw), bf),
            pltpu.VMEM((rows, HD), jnp.float32),
            pltpu.VMEM((rows, HD), jnp.float32),
            pltpu.VMEM((sources, kvl, PAGE, HD), bf),
            pltpu.VMEM((sources, kvl, PAGE, HD), bf),
            pltpu.VMEM((sources, kvl, PAGE, HD), bf),
            pltpu.VMEM((sources, kvl, PAGE, HD), bf),
            dma((3, kvl, ulysses - 1)),
            dma((3, kvl, ulysses - 1)),
            dma((3, kvl)),
            dma((2, kvl, hops)),
            dma((2, kvl, hops)),
            dma((2, sources - 1)),
            dma((2, sources - 1)),
            dma((2,)),
            dma((kvl, ulysses - 1)),
            dma((kvl, ulysses - 1)),
            dma((kvl,)),
        ],
        compiler_params=pltpu.CompilerParams(collective_id=0, has_side_effects=True),
    )(queries[0], keys[0], values[0], freq, request_pages, page_table)
    return (attended[None], cache_keys, cache_values)


def solution(mesh):
    in_specs = (
        P(("groups", "handoff"), ("blk", "ulysses"), None),
        P(("groups", "handoff"), ("blk", "ulysses"), None),
        P(("groups", "handoff"), ("blk", "ulysses"), None),
        P("groups", None),
        P("groups", None),
    )
    out_specs = (
        P(("groups", "handoff"), ("blk", "ulysses"), None),
        P(("groups", "blk", "handoff"), "ulysses", None, None),
        P(("groups", "blk", "handoff"), "ulysses", None, None),
    )
    return jax.shard_map(body, mesh=mesh, in_specs=in_specs, out_specs=out_specs, check_vma=False)
```

time: 88.3 us -> 47.8 us (0.54)
  Pallas kernels: 0 us -> 43.2 us
  waiting for transfers between devices: 27.5 us -> 0 us
  starting transfers between devices: 24.5 us -> 0 us
  local copies, waits for them, and re-layouts: 19.2 us -> 3.66 us
  loops' own time: 6.61 us -> 0 us
  other arithmetic: 6.52 us -> 0 us
  matrix products: 2.22 us -> 0 us
    pallas_call x0 -> x1, Pallas kernels: none -> 43.2 us  [body(): pl.pallas_call(functools.partial(kernel, sizes), out_shape=(jax.ShapeDtyp...]
    all_to_all x5 -> x0, waiting for transfers between devices: 27.5 us -> none  [the longest x1 12 us: body(): lax.all_to_all(outgoing_heads, 'ulysses', split_axis=0, concat_axis=2, ti...]
    all_to_all x5 -> x0, starting transfers between devices: 20.3 us -> none  [the longest x1 6.48 us: body(): lax.all_to_all(key_split, 'ulysses', split_axis=1, concat_axis=0, tiled=T...]
    another operation x1 -> x0, loops' own time: 6.61 us -> none  [body(): blocks = lax.map(attend, starts)]
    another operation x9 -> x0, local copies, waits for them, and re-layouts: 4.33 us -> none  [the longest x2 1.93 us: body(): key_split = keys[0].reshape(local_rows, ulysses_size, kv_local * HD)]
    ppermute x1 -> x0, starting transfers between devices: 4.21 us -> none  [from_behind(): return lax.ppermute(block, axis, route)]
    gather x3 -> x0, local copies, waits for them, and re-layouts: 3.96 us -> none  [the longest x1 1.4 us: body(): paged = local_kv.reshape(2, slots_dev, PAGE, kv_local, HD)[:, send_order]]
    reshape x5 -> x0, local copies, waits for them, and re-layouts: 3.56 us -> none  [the longest x1 2.21 us: body(): blocks.reshape(ulysses_size, local_rows, 1, kv_local * group_size * HD)]
  transfers between devices with their start and end apart: 6 -> 0, of which waited for: 4 -> 0; matrix products, arithmetic and copies ran while one was open for 25% -> 0% of each run, Pallas kernels for 0% -> 0%
where the time goes in v2:
time: 47.8 us; the launch traced here: 47.5 us
  Pallas kernels  43.2 us (90%)
  local copies, waits for them, and re-layouts  3.66 us (8%)
  between operations  0.65 us (1%)
    pallas_call x1, Pallas kernels, body(): pl.pallas_call(functools.partial(kernel, sizes), out_shape=(jax.ShapeDtyp...  43.2 us
    unnamed x7, local copies, waits for them, and re-layouts  3.66 us

profile of v2, /device:TPU:0, one launch (start us, length us, event | category | flops | bytes accessed | tf_op | source)
XLA Modules:
  0.0 47.5 jit_solution(2581349360462315663)
XLA Ops:
  0.6 43.2 %shard_map.85 = (bf16[64,4096]{1,0:T(8,128)(2,1)}, bf16[4,4,64,128]{3,2,1,0:T(8,128)(2,1)}, bf16[4,4,64,128]{3,2,1,0:T(8,128)(2,1)}) custom-call(bf16[64,4096]{1,0:T(8,128)(2,1)} %bitcast.5, bf16[64,2048]{1,0:T(8,128)(2,1)} %bitcast.6, bf16[64,2048]{1,0:T(8,128)(2,1)} %bitcast.7, f32[1,128]{1,0:T(1,128)} %constant.2.clone.freq_ref, s32[2,4]{1,0:T(2,128)} %pages_ref.1, ...), custom_call_target="tpu_custom_call" | custom-call | tf_op jit(solution)/shard_map/pallas_call | solution.py:321
  43.9 0.0 copy-start.1
  43.9 1.9 %copy.12 = bf16[1,64,4096]{2,1,0:T(8,128)(2,1)} copy(bf16[1,64,4096]{2,1,0:T(8,128)(2,1)} %bitcast.4) | data formatting | bytes 1048576
  45.8 0.0 copy-done.1
  45.8 0.0 copy-start
  45.8 0.7 %copy.13 = bf16[4,4,64,128]{3,2,1,0:T(8,128)(2,1)} copy(bf16[4,4,64,128]{3,2,1,0:T(8,128)(2,1)S(1)} %copy-done.1) | data formatting | bytes 524288
  46.5 0.3 copy-done
  46.8 0.7 %copy.14 = bf16[4,4,64,128]{3,2,1,0:T(8,128)(2,1)} copy(bf16[4,4,64,128]{3,2,1,0:T(8,128)(2,1)S(1)} %copy-done) | data formatting | bytes 524288
Async XLA Ops:
  43.9 1.9 %copy-start.1 = (bf16[4,4,64,128]{3,2,1,0:T(8,128)(2,1)S(1)}, bf16[4,4,64,128]{3,2,1,0:T(8,128)(2,1)}, u32[]{:S(2)}) copy-start(bf16[4,4,64,128]{3,2,1,0:T(8,128)(2,1)} %get-tuple-element.13) | copy-start | bytes 786436
  45.8 1.0 %copy-start = (bf16[4,4,64,128]{3,2,1,0:T(8,128)(2,1)S(1)}, bf16[4,4,64,128]{3,2,1,0:T(8,128)(2,1)}, u32[]{:S(2)}) copy-start(bf16[4,4,64,128]{3,2,1,0:T(8,128)(2,1)} %get-tuple-element.14) | copy-start | bytes 786436

commit v3 on v2

--- a/solution.py
+++ b/solution.py
@@ -34,8 +34,8 @@
 
 def kernel(
     sizes, q_ref, k_ref, v_ref, freq_ref, pages_ref, table_ref,
-    out_ref, ck_ref, cv_ref,
-    kraw, tab_k, tab_v, qbuf, obuf, cos_t, sin_t, out_k, out_v, got_k, got_v,
+    out_ref, got_k, got_v,
+    kraw, tab_k, tab_v, qbuf, obuf, cos_t, sin_t, out_k, out_v,
     in_send, in_recv, in_local, x_send, x_recv, c_send, c_recv, c_local, o_send, o_recv, o_local,
 ):
     ulysses, blks, cores, local, kvl, group, reach, reqs = sizes
@@ -266,15 +266,6 @@
     for i in range(1, sources):
         handed(0, i).wait_recv()
         handed(1, i).wait_recv()
-    for j in range(slots):
-        def step(n, found, j=j):
-            s = n // slots
-            page = table_ref[lax.rem(s, cores), (s // cores) * slots + lax.rem(n, slots)]
-            return found + jnp.where(page == mine * slots + j, s, 0)
-        source = lax.fori_loop(0, sources * slots, step, jnp.int32(0))
-        ck_ref[j] = pick(source, [got_k[s] for s in range(sources)])
-        cv_ref[j] = pick(source, [got_v[s] for s in range(sources)])
-
     for i in range(1, sources):
         handed(0, i).wait_send()
         handed(1, i).wait_send()
@@ -291,6 +282,25 @@
         own_out(h).wait()
         for i in range(1, ulysses):
             outgoing(h, i).wait()
+
+
+def place(sizes, table_ref, got_k, got_v, att_ref, out_ref, ck_ref, cv_ref, sem):
+    blks, cores, slots = sizes
+    sources = blks * cores
+    mine = lax.axis_index("blk") * cores + lax.axis_index("handoff")
+    copies = [pltpu.make_async_copy(att_ref, out_ref, sem.at[2 * slots])]
+    copies[0].start()
+    for j in range(slots):
+        def step(n, found, j=j):
+            s = n // slots
+            page = table_ref[lax.rem(s, cores), (s // cores) * slots + lax.rem(n, slots)]
+            return found + jnp.where(page == mine * slots + j, s, 0)
+        source = lax.fori_loop(0, sources * slots, step, jnp.int32(0))
+        for which, (got, cache) in enumerate(((got_k, ck_ref), (got_v, cv_ref))):
+            copies.append(pltpu.make_async_copy(got.at[source], cache.at[j], sem.at[2 * j + which]))
+            copies[-1].start()
+    for copy in copies:
+        copy.wait()
 
 
 def body(queries, keys, values, request_pages, page_table):
@@ -318,15 +328,15 @@
     anywhere = pl.BlockSpec(memory_space=pl.ANY)
     vmem = pl.BlockSpec(memory_space=pltpu.VMEM)
     smem = pl.BlockSpec(memory_space=pltpu.SMEM)
-    attended, cache_keys, cache_values = pl.pallas_call(
+    moved, pages_k, pages_v = pl.pallas_call(
         functools.partial(kernel, sizes),
         out_shape=(
-            jax.ShapeDtypeStruct((local, QH * HD), bf),
-            jax.ShapeDtypeStruct((slots, kvl, PAGE, HD), bf),
-            jax.ShapeDtypeStruct((slots, kvl, PAGE, HD), bf),
+            pltpu.VMEM((local, QH * HD), bf),
+            pltpu.VMEM((sources, kvl, PAGE, HD), bf),
+            pltpu.VMEM((sources, kvl, PAGE, HD), bf),
         ),
         in_specs=[anywhere, anywhere, anywhere, vmem, smem, smem],
-        out_specs=(anywhere, vmem, vmem),
+        out_specs=(vmem, vmem, vmem),
         scratch_shapes=[
             pltpu.VMEM((kvl, rows, HD), bf),
             pltpu.VMEM((kvl, (back + 1) * rows, HD), bf),
@@ -335,8 +345,6 @@
             pltpu.VMEM((kvl, rows, qw), bf),
             pltpu.VMEM((rows, HD), jnp.float32),
             pltpu.VMEM((rows, HD), jnp.float32),
-            pltpu.VMEM((sources, kvl, PAGE, HD), bf),
-            pltpu.VMEM((sources, kvl, PAGE, HD), bf),
             pltpu.VMEM((sources, kvl, PAGE, HD), bf),
             pltpu.VMEM((sources, kvl, PAGE, HD), bf),
             dma((3, kvl, ulysses - 1)),
@@ -353,6 +361,21 @@
         ],
         compiler_params=pltpu.CompilerParams(collective_id=0, has_side_effects=True),
     )(queries[0], keys[0], values[0], freq, request_pages, page_table)
+    pages_k, pages_v, moved = (
+        pltpu.with_memory_space_constraint(x, pltpu.VMEM) for x in (pages_k, pages_v, moved)
+    )
+    attended, cache_keys, cache_values = pl.pallas_call(
+        functools.partial(place, (blks, cores, slots)),
+        out_shape=(
+            jax.ShapeDtypeStruct((local, QH * HD), bf),
+            jax.ShapeDtypeStruct((slots, kvl, PAGE, HD), bf),
+            jax.ShapeDtypeStruct((slots, kvl, PAGE, HD), bf),
+        ),
+        in_specs=[smem, anywhere, anywhere, anywhere],
+        out_specs=(anywhere, anywhere, anywhere),
+        scratch_shapes=[dma((2 * slots + 1,))],
+        compiler_params=pltpu.CompilerParams(vmem_limit_bytes=1 << 20),
+    )(page_table, pages_k, pages_v, moved)
     return (attended[None], cache_keys, cache_values)
 
 

time: 47.8 us -> 46.5 us (0.973)
  local copies, waits for them, and re-layouts: 3.66 us -> 0.67 us
  Pallas kernels: 43.2 us -> 45 us
    unnamed x7 -> x2, local copies, waits for them, and re-layouts: 3.66 us -> 0.67 us
    pallas_call x1 -> x2, Pallas kernels: 43.2 us -> 45 us  [the longest x1 42.3 us: body(): pl.pallas_call(functools.partial(kernel, sizes), out_shape=(pltpu.VMEM((l...]
where the time goes in v3:
time: 46.5 us; the launch traced here: 46.3 us
  Pallas kernels  45 us (97%)
  local copies, waits for them, and re-layouts  0.67 us (1%)
  between operations  0.65 us (1%)
    pallas_call x1, Pallas kernels, body(): pl.pallas_call(functools.partial(kernel, sizes), out_shape=(pltpu.VMEM((l...  42.3 us
    pallas_call x1, Pallas kernels, body(): pl.pallas_call(functools.partial(place, (blks, cores, slots)), out_shape=...  2.68 us

profile of v3, /device:TPU:0, one launch (start us, length us, event | category | flops | bytes accessed | tf_op | source)
XLA Modules:
  0.0 46.3 jit_solution(8898170706147061591)
XLA Ops:
  0.6 42.3 %shard_map.85 = (bf16[64,4096]{1,0:T(8,128)(2,1)S(1)}, bf16[4,4,64,128]{3,2,1,0:T(8,128)(2,1)S(1)}, bf16[4,4,64,128]{3,2,1,0:T(8,128)(2,1)S(1)}) custom-call(bf16[64,4096]{1,0:T(8,128)(2,1)} %bitcast.4, bf16[64,2048]{1,0:T(8,128)(2,1)} %bitcast.5, bf16[64,2048]{1,0:T(8,128)(2,1)} %bitcast.6, f32[1,128]{1,0:T(1,128)} %constant.2.clone.freq_ref, ...), custom_call_target="tpu_custom_call" | custom-call | tf_op jit(solution)/shard_map/pallas_call | solution.py:331
  43.0 0.0 copy-start
  43.0 0.7 %copy-done = s32[2,8]{1,0:T(2,128)S(1)} copy-done((s32[2,8]{1,0:T(2,128)S(1)}, s32[2,8]{1,0:T(2,128)}, u32[]{:S(2)}) %copy-start) | copy-done | bytes 88
  43.6 2.7 %shard_map.86 = (bf16[64,4096]{1,0:T(8,128)(2,1)}, bf16[4,4,64,128]{3,2,1,0:T(8,128)(2,1)}, bf16[4,4,64,128]{3,2,1,0:T(8,128)(2,1)}) custom-call(s32[2,8]{1,0:T(2,128)S(1)} %copy-done, bf16[4,4,64,128]{3,2,1,0:T(8,128)(2,1)S(1)} %get-tuple-element.9.got_k, bf16[4,4,64,128]{3,2,1,0:T(8,128)(2,1)S(1)} %get-tuple-element.10.got_v, ...), custom_call_target="tpu_custom_call" | custom-call | tf_op jit(solution)/shard_map/pallas_call | solution.py:367
Async XLA Ops:
  43.0 0.7 %copy-start = (s32[2,8]{1,0:T(2,128)S(1)}, s32[2,8]{1,0:T(2,128)}, u32[]{:S(2)}) copy-start(s32[2,8]{1,0:T(2,128)} %table_ref.3) | copy-start | bytes 196

commit v4 on v2

--- a/solution.py
+++ b/solution.py
@@ -291,6 +291,16 @@
         own_out(h).wait()
         for i in range(1, ulysses):
             outgoing(h, i).wait()
+
+
+def place(*refs):
+    count = (len(refs) - 1) // 2
+    sem = refs[-1]
+    copies = [pltpu.make_async_copy(refs[i], refs[count + i], sem.at[i]) for i in range(count)]
+    for copy in copies:
+        copy.start()
+    for copy in copies:
+        copy.wait()
 
 
 def body(queries, keys, values, request_pages, page_table):
@@ -318,15 +328,15 @@
     anywhere = pl.BlockSpec(memory_space=pl.ANY)
     vmem = pl.BlockSpec(memory_space=pltpu.VMEM)
     smem = pl.BlockSpec(memory_space=pltpu.SMEM)
-    attended, cache_keys, cache_values = pl.pallas_call(
+    results = pl.pallas_call(
         functools.partial(kernel, sizes),
         out_shape=(
-            jax.ShapeDtypeStruct((local, QH * HD), bf),
-            jax.ShapeDtypeStruct((slots, kvl, PAGE, HD), bf),
-            jax.ShapeDtypeStruct((slots, kvl, PAGE, HD), bf),
+            pltpu.VMEM((local, QH * HD), bf),
+            pltpu.VMEM((slots, kvl, PAGE, HD), bf),
+            pltpu.VMEM((slots, kvl, PAGE, HD), bf),
         ),
         in_specs=[anywhere, anywhere, anywhere, vmem, smem, smem],
-        out_specs=(anywhere, vmem, vmem),
+        out_specs=(vmem, vmem, vmem),
         scratch_shapes=[
             pltpu.VMEM((kvl, rows, HD), bf),
             pltpu.VMEM((kvl, (back + 1) * rows, HD), bf),
@@ -353,6 +363,15 @@
         ],
         compiler_params=pltpu.CompilerParams(collective_id=0, has_side_effects=True),
     )(queries[0], keys[0], values[0], freq, request_pages, page_table)
+    results = [pltpu.with_memory_space_constraint(x, pltpu.VMEM) for x in results]
+    attended, cache_keys, cache_values = pl.pallas_call(
+        place,
+        out_shape=tuple(jax.ShapeDtypeStruct(x.shape, x.dtype) for x in results),
+        in_specs=[anywhere] * len(results),
+        out_specs=(anywhere,) * len(results),
+        scratch_shapes=[dma((len(results),))],
+        compiler_params=pltpu.CompilerParams(vmem_limit_bytes=1 << 20),
+    )(*results)
     return (attended[None], cache_keys, cache_values)
 
 

time: 47.8 us -> 44.1 us (0.923)
  local copies, waits for them, and re-layouts: 3.66 us -> 0 us
    unnamed x7 -> x0, local copies, waits for them, and re-layouts: 3.66 us -> none
    pallas_call x1 -> x2, Pallas kernels: 43.2 us -> 43.3 us  [the longest x1 42.3 us: body(): pl.pallas_call(functools.partial(kernel, sizes), out_shape=(pltpu.VMEM((l...]
where the time goes in v4:
time: 44.1 us; the launch traced here: 43.9 us
  Pallas kernels  43.3 us (98%)
  between operations  0.64 us (1%)
    pallas_call x1, Pallas kernels, body(): pl.pallas_call(functools.partial(kernel, sizes), out_shape=(pltpu.VMEM((l...  42.3 us
    pallas_call x1, Pallas kernels, body(): pl.pallas_call(place, out_shape=tuple((jax.ShapeDtypeStruct(x.shape, x.dt...  0.99 us

profile of v4, /device:TPU:0, one launch (start us, length us, event | category | flops | bytes accessed | tf_op | source)
XLA Modules:
  0.0 43.9 jit_solution(15272320975671365615)
XLA Ops:
  0.6 42.3 %shard_map.85 = (bf16[64,4096]{1,0:T(8,128)(2,1)S(1)}, bf16[4,4,64,128]{3,2,1,0:T(8,128)(2,1)S(1)}, bf16[4,4,64,128]{3,2,1,0:T(8,128)(2,1)S(1)}) custom-call(bf16[64,4096]{1,0:T(8,128)(2,1)} %bitcast.4, bf16[64,2048]{1,0:T(8,128)(2,1)} %bitcast.5, bf16[64,2048]{1,0:T(8,128)(2,1)} %bitcast.6, f32[1,128]{1,0:T(1,128)} %constant.2.clone.freq_ref, ...), custom_call_target="tpu_custom_call" | custom-call | tf_op jit(solution)/shard_map/pallas_call | solution.py:331
  43.0 1.0 %shard_map.86 = (bf16[64,4096]{1,0:T(8,128)(2,1)}, bf16[4,4,64,128]{3,2,1,0:T(8,128)(2,1)}, bf16[4,4,64,128]{3,2,1,0:T(8,128)(2,1)}) custom-call(bf16[64,4096]{1,0:T(8,128)(2,1)S(1)} %get-tuple-element.9.refs_0_, bf16[4,4,64,128]{3,2,1,0:T(8,128)(2,1)S(1)} %get-tuple-element.10.refs_1_, bf16[4,4,64,128]{3,2,1,0:T(8,128)(2,1)S(1)} %get-tuple-element.11.refs_2_), custom_call_target="tpu_custom_call" | custom-call | tf_op jit(solution)/shard_map/pallas_call | solution.py:367

commit v5 on v4

--- a/solution.py
+++ b/solution.py
@@ -291,6 +291,337 @@
         own_out(h).wait()
         for i in range(1, ulysses):
             outgoing(h, i).wait()
+
+
+def near_kernel(
+    sizes, q_ref, k_ref, v_ref, freq_ref, pages_ref, table_ref,
+    out_ref, ck_ref, cv_ref,
+    kraw, tab_k, tab_v, qbuf, obuf, cos_t, sin_t, out_k, out_v, got_k, got_v,
+    in_send, in_recv, in_local, x_send, x_recv, c_send, c_recv, c_local, o_send, o_recv, o_local,
+):
+    ulysses, blks, cores, local, kvl, group, reach, reqs = sizes
+    rows = ulysses * local
+    slots = rows // PAGE
+    sources = blks * cores
+    back = min(-(-reach // rows), blks - 1)
+    home = back * rows
+    half = ulysses // 2
+    part = half * local
+    qw = group * HD
+    me = lax.axis_index("ulysses")
+    blk = lax.axis_index("blk")
+    pack = lax.axis_index("handoff")
+    mine = blk * cores + pack
+    side = me // half
+    member = lax.rem(me, half)
+    diagonal = back > 0
+
+    def quarter(a, device):
+        return device if a == 0 else lax.rem(device + half, ulysses)
+
+    def h_peer(i):
+        return side * half + lax.rem(member + i, half)
+
+    barrier = pltpu.get_barrier_semaphore()
+
+    def u_peer(i):
+        return lax.rem(me + i, ulysses)
+
+    def s_peer(i):
+        p = lax.rem(mine + i, sources)
+        return p, {"blk": p // cores, "handoff": lax.rem(p, cores)}
+
+    for i in range(1, ulysses):
+        pl.semaphore_signal(barrier, inc=1, device_id={"ulysses": u_peer(i)}, device_id_type=MESH)
+    for i in range(1, sources):
+        pl.semaphore_signal(barrier, inc=1, device_id=s_peer(i)[1], device_id_type=MESH)
+
+    if diagonal:
+        @pl.when((side == 0) & (blk > 0))
+        def _():
+            pl.semaphore_signal(
+                barrier, inc=1, device_id={"blk": lax.rem(blk + blks - 1, blks), "ulysses": quarter(1, me)},
+                device_id_type=MESH,
+            )
+
+    for hop in range(1, back + 1):
+        @pl.when(blk < hop)
+        def _():
+            gap = pl.ds((back - hop) * rows, rows)
+            tab_k[:, :, gap, :] = jnp.zeros((2, kvl, rows, HD), jnp.bfloat16)
+            tab_v[:, :, gap, :] = jnp.zeros((2, kvl, rows, HD), jnp.bfloat16)
+
+    greeted = ulysses - 1 + sources - 1
+    if diagonal:
+        awaited = (side == 1) & (blk + 1 < blks)
+
+        @pl.when(awaited)
+        def _():
+            pl.semaphore_wait(barrier, greeted + 1)
+
+        @pl.when(jnp.logical_not(awaited))
+        def _():
+            pl.semaphore_wait(barrier, greeted)
+    else:
+        pl.semaphore_wait(barrier, greeted)
+
+    def landing(what, a, h, whose):
+        if what == 0:
+            return kraw.at[a, h, pl.ds(whose * local, local), :]
+        if what == 1:
+            return tab_v.at[a, h, pl.ds(home + whose * local, local), :]
+        return qbuf.at[a, h, pl.ds(lax.rem(whose, half) * local, local), :]
+
+    def leaving(what, a, h, whose):
+        width = qw if what == 2 else HD
+        ref = (k_ref, v_ref, q_ref)[what]
+        return ref.at[:, pl.ds(pl.multiple_of((quarter(a, whose) * kvl + h) * width, width), width)]
+
+    def incoming(what, a, h, i):
+        peer = h_peer(i) if what == 2 else u_peer(i)
+        return pltpu.make_async_remote_copy(
+            src_ref=leaving(what, a, h, peer), dst_ref=landing(what, a, h, me),
+            send_sem=in_send.at[what, a, h, i - 1], recv_sem=in_recv.at[what, a, h, i - 1],
+            device_id={"ulysses": peer}, device_id_type=MESH,
+        )
+
+    def own_in(what, a, h):
+        return pltpu.make_async_copy(
+            leaving(what, a, h, me), landing(what, a, h, me), in_local.at[what, a, h]
+        )
+
+    def each_send(what, a, act):
+        for i in range(1, half if what == 2 else ulysses):
+            if what == 2 or a == 0:
+                act(i)
+            else:
+                @pl.when(u_peer(i) // half >= side)
+                def _(i=i):
+                    act(i)
+
+    def each_receive(what, a, act):
+        for i in range(1, half if what == 2 else ulysses):
+            if what == 2 or a == 0:
+                act(i)
+            else:
+                @pl.when(lax.rem(me + ulysses - i, ulysses) // half <= side)
+                def _(i=i):
+                    act(i)
+
+    order = [(w, a, h) for a in (0, 1) for h in range(kvl) for w in (0, 1)]
+    order += [(2, a, h) for a in (0, 1) for h in range(kvl)]
+    for what, a, h in order:
+        each_send(what, a, lambda i, what=what, a=a, h=h: incoming(what, a, h, i).start())
+        own_in(what, a, h).start()
+
+    def arrive(what, a, h):
+        own_in(what, a, h).wait()
+        each_receive(what, a, lambda i: incoming(what, a, h, i).wait_recv())
+
+    ends = []
+    starts = []
+    total = jnp.int32(0)
+    for r in range(reqs):
+        starts.append(total)
+        total = total + pages_ref[pack, r] * PAGE
+        ends.append(total)
+
+    def first_token(pos):
+        first = jnp.zeros_like(pos)
+        for r in range(reqs):
+            first = jnp.maximum(first, jnp.where(pos >= starts[r], starts[r], 0))
+        return first
+
+    pos_rows = blk * rows + lax.broadcasted_iota(jnp.int32, (rows, HD), 0)
+    rel = (pos_rows - first_token(pos_rows)).astype(jnp.float32)
+    angles = rel * freq_ref[...]
+    lanes = lax.broadcasted_iota(jnp.int32, (rows, HD), 1)
+    cos_t[...] = jnp.cos(angles)
+    sine = jnp.sin(angles)
+    sin_t[...] = jnp.where(lanes < HD // 2, -sine, sine)
+
+    def onward(kind, which, h):
+        tab = (tab_k, tab_v)[which]
+        begin, length = (0, rows) if kind == 0 else (side * part, part)
+        source = 1 if kind == 1 else 0
+        target = 0 if kind == 0 else 1
+        device = {"blk": lax.rem(blk + 1, blks)}
+        if kind == 2:
+            device["ulysses"] = quarter(1, me)
+            begin = part
+        return pltpu.make_async_remote_copy(
+            src_ref=tab.at[source, h, pl.ds(home + begin, length), :],
+            dst_ref=tab.at[target, h, pl.ds(begin, length), :],
+            send_sem=x_send.at[kind, which, h], recv_sem=x_recv.at[kind, which, h],
+            device_id=device, device_id_type=MESH,
+        )
+
+    for a in (0, 1):
+        for h in range(kvl):
+            arrive(0, a, h)
+            first = rows if a == 0 else part
+            tab_k[a, h, pl.ds(home, first), :] = turn(
+                kraw[a, h, pl.ds(0, first), :], cos_t[pl.ds(0, first), :], sin_t[pl.ds(0, first), :]
+            )
+            if a == 1:
+                @pl.when(side == 1)
+                def _(h=h):
+                    rest = pl.ds(part, part)
+                    tab_k[1, h, pl.ds(home + part, part), :] = turn(
+                        kraw[1, h, rest, :], cos_t[rest, :], sin_t[rest, :]
+                    )
+            arrive(1, a, h)
+            if diagonal:
+                @pl.when(blk + 1 < blks)
+                def _(a=a, h=h):
+                    onward(a, 0, h).start()
+                    onward(a, 1, h).start()
+                if a == 0:
+                    @pl.when((blk + 1 < blks) & (side == 1))
+                    def _(h=h):
+                        onward(2, 0, h).start()
+                        onward(2, 1, h).start()
+
+    def page_for(owner):
+        def step(j, found):
+            page = table_ref[pack, blk * slots + j]
+            return found + jnp.where(lax.div(page, jnp.int32(slots)) == owner, j, 0)
+        return lax.fori_loop(0, slots, step, jnp.int32(0))
+
+    def handed(which, i):
+        src, dst = ((out_k, got_k), (out_v, got_v))[which]
+        return pltpu.make_async_remote_copy(
+            src_ref=src.at[i], dst_ref=dst.at[mine],
+            send_sem=c_send.at[which, i - 1], recv_sem=c_recv.at[which, i - 1],
+            device_id=s_peer(i)[1], device_id_type=MESH,
+        )
+
+    def own_page(which):
+        src, dst = ((out_k, got_k), (out_v, got_v))[which]
+        return pltpu.make_async_copy(src.at[0], dst.at[mine], c_local.at[which])
+
+    for i in range(sources):
+        chosen = page_for(s_peer(i)[0])
+        for tab, out in ((tab_k, out_k), (tab_v, out_v)):
+            out[i] = pick(chosen, [tab[0, :, home + j * PAGE:home + (j + 1) * PAGE, :] for j in range(slots)])
+    for i in range(1, sources):
+        handed(0, i).start()
+        handed(1, i).start()
+    own_page(0).start()
+    own_page(1).start()
+
+    block = part
+    lead = min(-(-reach // block) * block, home)
+    span = lead + block
+    chunk = span
+    factor = QUERY_SCALE / SOFT_CAP
+
+    def attend(a, h, at):
+        here = pl.ds(at, block)
+        cosine, sine_here = cos_t[here, :], sin_t[here, :]
+        query = jnp.concatenate(
+            [turn(qbuf[a, h, :, g * HD:(g + 1) * HD], cosine, sine_here) for g in range(group)], axis=0
+        )
+        pos = blk * rows + at + lax.broadcasted_iota(jnp.int32, (block, 1), 0)
+        low = jnp.maximum(first_token(pos), pos - (WINDOW - 1))
+        pos = jnp.concatenate([pos] * group, axis=0)
+        low = jnp.concatenate([low] * group, axis=0)
+        begin = home + at - lead
+
+        def piece():
+            start = begin
+            seen = pl.ds(start, chunk)
+            scores = lax.dot_general(
+                query, tab_k[a, h, seen, :], (((1,), (1,)), ((), ())), preferred_element_type=jnp.float32
+            )
+            weights = jnp.exp(SOFT_CAP * jnp.tanh(scores * factor))
+            key_pos = (blk - back) * rows + start + lax.broadcasted_iota(jnp.int32, (1, chunk), 1)
+            weights = jnp.where((key_pos <= pos) & (key_pos >= low), weights, 0.0)
+            total = jnp.sum(weights, axis=1, keepdims=True)
+            mixed = jnp.dot(
+                weights.astype(jnp.bfloat16), tab_v[a, h, seen, :], preferred_element_type=jnp.float32
+            )
+            return mixed, total
+
+        mixed, total = piece()
+        result = (mixed / total).astype(jnp.bfloat16)
+        for g in range(group):
+            obuf[a, h, :, g * HD:(g + 1) * HD] = result[g * block:(g + 1) * block]
+
+    def columns(a, h):
+        return out_ref.at[:, pl.ds(pl.multiple_of((quarter(a, me) * kvl + h) * qw, qw), qw)]
+
+    def finished(a, h, device):
+        start = pl.multiple_of(lax.rem(device, half) * local, local)
+        return obuf.at[a, h, pl.ds(start, local), :]
+
+    def outgoing(a, h, i):
+        return pltpu.make_async_remote_copy(
+            src_ref=finished(a, h, h_peer(i)), dst_ref=columns(a, h),
+            send_sem=o_send.at[a, h, i - 1], recv_sem=o_recv.at[a, h, i - 1],
+            device_id={"ulysses": h_peer(i)}, device_id_type=MESH,
+        )
+
+    def own_out(a, h):
+        return pltpu.make_async_copy(finished(a, h, me), columns(a, h), o_local.at[a, h])
+
+    for a in (0, 1):
+        for h in range(kvl):
+            if diagonal:
+                @pl.when(blk > 0)
+                def _(a=a, h=h):
+                    onward(a, 0, h).wait_recv()
+                    onward(a, 1, h).wait_recv()
+                if a == 1:
+                    @pl.when((blk > 0) & (side == 0))
+                    def _(h=h):
+                        onward(2, 0, h).wait_recv()
+                        onward(2, 1, h).wait_recv()
+            arrive(2, a, h)
+            for where in (0, 1):
+                @pl.when(side == where)
+                def _(a=a, h=h, where=where):
+                    attend(a, h, where * part)
+            for i in range(1, half):
+                outgoing(a, h, i).start()
+            own_out(a, h).start()
+
+    own_page(0).wait()
+    own_page(1).wait()
+    for i in range(1, sources):
+        handed(0, i).wait_recv()
+        handed(1, i).wait_recv()
+    for j in range(slots):
+        def step(n, found, j=j):
+            s = n // slots
+            page = table_ref[lax.rem(s, cores), (s // cores) * slots + lax.rem(n, slots)]
+            return found + jnp.where(page == mine * slots + j, s, 0)
+        source = lax.fori_loop(0, sources * slots, step, jnp.int32(0))
+        ck_ref[j] = pick(source, [got_k[s] for s in range(sources)])
+        cv_ref[j] = pick(source, [got_v[s] for s in range(sources)])
+
+    for i in range(1, sources):
+        handed(0, i).wait_send()
+        handed(1, i).wait_send()
+    for what, a, h in order:
+        each_send(what, a, lambda i, what=what, a=a, h=h: incoming(what, a, h, i).wait_send())
+    for h in range(kvl):
+        if diagonal:
+            @pl.when(blk + 1 < blks)
+            def _(h=h):
+                for kind in (0, 1):
+                    onward(kind, 0, h).wait_send()
+                    onward(kind, 1, h).wait_send()
+
+            @pl.when((blk + 1 < blks) & (side == 1))
+            def _(h=h):
+                onward(2, 0, h).wait_send()
+                onward(2, 1, h).wait_send()
+    for a in (0, 1):
+        for h in range(kvl):
+            own_out(a, h).wait()
+            for i in range(1, half):
+                outgoing(a, h, i).wait()
 
 
 def place(*refs):
@@ -325,11 +656,15 @@
     bf = jnp.bfloat16
     dma = pltpu.SemaphoreType.DMA
     hops = max(back, 1)
+    near = reach <= rows and ulysses % 2 == 0 and ulysses > 2
+    sets = (2,) if near else ()
+    mates = (ulysses // 2 if near else ulysses) - 1
+    asked = mates + 1 if near else ulysses
     anywhere = pl.BlockSpec(memory_space=pl.ANY)
     vmem = pl.BlockSpec(memory_space=pltpu.VMEM)
     smem = pl.BlockSpec(memory_space=pltpu.SMEM)
     results = pl.pallas_call(
-        functools.partial(kernel, sizes),
+        functools.partial(near_kernel if near else kernel, sizes),
         out_shape=(
             pltpu.VMEM((local, QH * HD), bf),
             pltpu.VMEM((slots, kvl, PAGE, HD), bf),
@@ -338,30 +673,30 @@
         in_specs=[anywhere, anywhere, anywhere, vmem, smem, smem],
         out_specs=(vmem, vmem, vmem),
         scratch_shapes=[
-            pltpu.VMEM((kvl, rows, HD), bf),
-            pltpu.VMEM((kvl, (back + 1) * rows, HD), bf),
-            pltpu.VMEM((kvl, (back + 1) * rows, HD), bf),
-            pltpu.VMEM((kvl, rows, qw), bf),
-            pltpu.VMEM((kvl, rows, qw), bf),
+            pltpu.VMEM(sets + (kvl, rows, HD), bf),
+            pltpu.VMEM(sets + (kvl, (back + 1) * rows, HD), bf),
+            pltpu.VMEM(sets + (kvl, (back + 1) * rows, HD), bf),
+            pltpu.VMEM(sets + (kvl, asked * local, qw), bf),
+            pltpu.VMEM(sets + (kvl, asked * local, qw), bf),
             pltpu.VMEM((rows, HD), jnp.float32),
             pltpu.VMEM((rows, HD), jnp.float32),
             pltpu.VMEM((sources, kvl, PAGE, HD), bf),
             pltpu.VMEM((sources, kvl, PAGE, HD), bf),
             pltpu.VMEM((sources, kvl, PAGE, HD), bf),
             pltpu.VMEM((sources, kvl, PAGE, HD), bf),
-            dma((3, kvl, ulysses - 1)),
-            dma((3, kvl, ulysses - 1)),
-            dma((3, kvl)),
-            dma((2, kvl, hops)),
-            dma((2, kvl, hops)),
+            dma((3,) + sets + (kvl, ulysses - 1)),
+            dma((3,) + sets + (kvl, ulysses - 1)),
+            dma((3,) + sets + (kvl,)),
+            dma((3, 2, kvl) if near else (2, kvl, hops)),
+            dma((3, 2, kvl) if near else (2, kvl, hops)),
             dma((2, sources - 1)),
             dma((2, sources - 1)),
             dma((2,)),
-            dma((kvl, ulysses - 1)),
-            dma((kvl, ulysses - 1)),
-            dma((kvl,)),
+            dma(sets + (kvl, mates)),
+            dma(sets + (kvl, mates)),
+            dma(sets + (kvl,)),
         ],
-        compiler_params=pltpu.CompilerParams(collective_id=0, has_side_effects=True),
+        compiler_params=pltpu.CompilerParams(collective_id=1 if near else 0, has_side_effects=True),
     )(queries[0], keys[0], values[0], freq, request_pages, page_table)
     results = [pltpu.with_memory_space_constraint(x, pltpu.VMEM) for x in results]
     attended, cache_keys, cache_values = pl.pallas_call(

time: 44.1 us -> 45.1 us (1.023)
  the two profiles are of different devices: /device:TPU:0 before, /device:TPU:3 now
where the time goes in v5:
time: 45.1 us; the launch traced here: 45 us
  Pallas kernels  44.3 us (98%)
  between operations  0.64 us (1%)
    pallas_call x1, Pallas kernels, body(): pl.pallas_call(functools.partial(near_kernel if near else kernel, sizes),...  43.4 us
    pallas_call x1, Pallas kernels, body(): pl.pallas_call(place, out_shape=tuple((jax.ShapeDtypeStruct(x.shape, x.dt...  0.99 us

profile of v5, /device:TPU:3, one launch (start us, length us, event | category | flops | bytes accessed | tf_op | source)
XLA Modules:
  0.0 45.0 jit_solution(1591013409918221720)
XLA Ops:
  0.6 43.4 %shard_map.85 = (bf16[64,4096]{1,0:T(8,128)(2,1)S(1)}, bf16[4,4,64,128]{3,2,1,0:T(8,128)(2,1)S(1)}, bf16[4,4,64,128]{3,2,1,0:T(8,128)(2,1)S(1)}) custom-call(bf16[64,4096]{1,0:T(8,128)(2,1)} %bitcast.4, bf16[64,2048]{1,0:T(8,128)(2,1)} %bitcast.5, bf16[64,2048]{1,0:T(8,128)(2,1)} %bitcast.6, f32[1,128]{1,0:T(1,128)} %constant.2.clone.freq_ref, ...), custom_call_target="tpu_custom_call" | custom-call | tf_op jit(solution)/shard_map/pallas_call | solution.py:666
  44.0 1.0 %shard_map.86 = (bf16[64,4096]{1,0:T(8,128)(2,1)}, bf16[4,4,64,128]{3,2,1,0:T(8,128)(2,1)}, bf16[4,4,64,128]{3,2,1,0:T(8,128)(2,1)}) custom-call(bf16[64,4096]{1,0:T(8,128)(2,1)S(1)} %get-tuple-element.9.refs_0_, bf16[4,4,64,128]{3,2,1,0:T(8,128)(2,1)S(1)} %get-tuple-element.10.refs_1_, bf16[4,4,64,128]{3,2,1,0:T(8,128)(2,1)S(1)} %get-tuple-element.11.refs_2_), custom_call_target="tpu_custom_call" | custom-call | tf_op jit(solution)/shard_map/pallas_call | solution.py:702

commit v6 on v5

--- a/solution.py
+++ b/solution.py
@@ -408,8 +408,10 @@
                 def _(i=i):
                     act(i)
 
-    order = [(w, a, h) for a in (0, 1) for h in range(kvl) for w in (0, 1)]
-    order += [(2, a, h) for a in (0, 1) for h in range(kvl)]
+    order = []
+    for a in (0, 1):
+        order += [(w, a, h) for h in range(kvl) for w in (0, 1)]
+        order += [(2, a, h) for h in range(kvl)]
     for what, a, h in order:
         each_send(what, a, lambda i, what=what, a=a, h=h: incoming(what, a, h, i).start())
         own_in(what, a, h).start()
@@ -456,7 +458,7 @@
             device_id=device, device_id_type=MESH,
         )
 
-    for a in (0, 1):
+    def intake(a):
         for h in range(kvl):
             arrive(0, a, h)
             first = rows if a == 0 else part
@@ -482,6 +484,8 @@
                         onward(2, 0, h).start()
                         onward(2, 1, h).start()
 
+    intake(0)
+
     def page_for(owner):
         def step(j, found):
             page = table_ref[pack, blk * slots + j]
@@ -565,7 +569,7 @@
     def own_out(a, h):
         return pltpu.make_async_copy(finished(a, h, me), columns(a, h), o_local.at[a, h])
 
-    for a in (0, 1):
+    def heads(a):
         for h in range(kvl):
             if diagonal:
                 @pl.when(blk > 0)
@@ -585,6 +589,10 @@
             for i in range(1, half):
                 outgoing(a, h, i).start()
             own_out(a, h).start()
+
+    heads(0)
+    intake(1)
+    heads(1)
 
     own_page(0).wait()
     own_page(1).wait()

time: 45.1 us -> 47.4 us (1.051)
  the two profiles are of different devices: /device:TPU:3 before, /device:TPU:2 now
where the time goes in v6:
time: 47.4 us; the launch traced here: 47.3 us
  Pallas kernels  46.6 us (98%)
  between operations  0.64 us (1%)
    pallas_call x1, Pallas kernels, body(): pl.pallas_call(functools.partial(near_kernel if near else kernel, sizes),...  45.6 us
    pallas_call x1, Pallas kernels, body(): pl.pallas_call(place, out_shape=tuple((jax.ShapeDtypeStruct(x.shape, x.dt...  0.99 us

profile of v6, /device:TPU:2, one launch (start us, length us, event | category | flops | bytes accessed | tf_op | source)
XLA Modules:
  0.0 47.3 jit_solution(4184412155952048465)
XLA Ops:
  0.6 45.6 %shard_map.85 = (bf16[64,4096]{1,0:T(8,128)(2,1)S(1)}, bf16[4,4,64,128]{3,2,1,0:T(8,128)(2,1)S(1)}, bf16[4,4,64,128]{3,2,1,0:T(8,128)(2,1)S(1)}) custom-call(bf16[64,4096]{1,0:T(8,128)(2,1)} %bitcast.4, bf16[64,2048]{1,0:T(8,128)(2,1)} %bitcast.5, bf16[64,2048]{1,0:T(8,128)(2,1)} %bitcast.6, f32[1,128]{1,0:T(1,128)} %constant.2.clone.freq_ref, ...), custom_call_target="tpu_custom_call" | custom-call | tf_op jit(solution)/shard_map/pallas_call | solution.py:674
  46.3 1.0 %shard_map.86 = (bf16[64,4096]{1,0:T(8,128)(2,1)}, bf16[4,4,64,128]{3,2,1,0:T(8,128)(2,1)}, bf16[4,4,64,128]{3,2,1,0:T(8,128)(2,1)}) custom-call(bf16[64,4096]{1,0:T(8,128)(2,1)S(1)} %get-tuple-element.9.refs_0_, bf16[4,4,64,128]{3,2,1,0:T(8,128)(2,1)S(1)} %get-tuple-element.10.refs_1_, bf16[4,4,64,128]{3,2,1,0:T(8,128)(2,1)S(1)} %get-tuple-element.11.refs_2_), custom_call_target="tpu_custom_call" | custom-call | tf_op jit(solution)/shard_map/pallas_call | solution.py:710
